TPU v7x, 32 devices: a whole 2x2x4 slice. The times are simulated.
32 devices in a mesh: head: 8 (over z, x), ctx: 4 (over y, core).
Axes of the slice: x: 2, y: 2, z: 4, core: 2. Of those that a mesh axis runs over, the one named last changes fastest.
Arguments:
- queries: bfloat16 [768, 16384], P('ctx', 'head'), may hold values from -12 to 12
- rotated_key_rows: bfloat16 [768, 1024], P('ctx'), may hold values from -5 to 5
- value_state_rows: bfloat16 [768, 1024], P('ctx'), may hold values from -6 to 6
- positions: int32 [768], P('ctx'), may hold values from 0 to 767, as said below
Outputs:
- attended: bfloat16 [768, 16384], P('ctx', 'head')
Inputs may be any that keep to these rules, and one draw needn't show every extreme that they name: Each aligned block of 96 rows holds 96 consecutive positions in ascending order; the blocks' starts are a permutation of the multiples of 96.
All inputs are finite; a program needn't handle non-finite values.
Results may differ from a plain program's by a relative error of at most 0.0054.
Values may be sent and summed in bfloat16 or wider, within the bound.
No kernel may reach another device: no remote copies, remote signals or barrier semaphores. Data moves between devices by JAX's collectives and lax.ppermute only.
A program may use at most 64 MiB of HBM per device.

v0:
```python
import jax
import jax.numpy as jnp
from jax import lax
from jax.sharding import PartitionSpec as P

HEAD_SIZE = 128
QUERIES_PER_KV = 16


negative_fill = -1e30


def shifted(block, axis, distance):
    devices = range(lax.axis_size(axis))
    route = [((i - distance) % len(devices), i) for i in devices]
    return lax.ppermute(block, axis, route)


def body(queries, rotated_key_rows, value_state_rows, positions):
    row_count = queries.shape[0]
    heads_here = queries.shape[1] // HEAD_SIZE
    query_view = queries.reshape(row_count, heads_here, HEAD_SIZE)
    group_index = lax.axis_index("head") * heads_here // QUERIES_PER_KV
    key_slice = lax.dynamic_slice_in_dim(rotated_key_rows, group_index * HEAD_SIZE, HEAD_SIZE, 1)
    value_slice = lax.dynamic_slice_in_dim(value_state_rows, group_index * HEAD_SIZE, HEAD_SIZE, 1)
    own_rows = jnp.concatenate([key_slice, value_slice], 1)
    scale_value = HEAD_SIZE ** (-0.5)

    def absorb(running, pair_rows, key_positions):
        highest, total, summed = running
        keys_part = pair_rows[:, :HEAD_SIZE]
        values_part = pair_rows[:, HEAD_SIZE:]
        scores = (
            jnp.einsum("rhd,kd->rhk", query_view, keys_part, preferred_element_type=jnp.float32)
            * scale_value
        )
        allowed = (key_positions[None, :] <= positions[:, None])[:, None, :]
        scores = jnp.where(allowed, scores, negative_fill)
        newest = jnp.maximum(highest, scores.max(-1))
        factor = jnp.exp(highest - newest)
        weights = jnp.where(allowed, jnp.exp(scores - newest[..., None]), 0.0)
        total = total * factor + weights.sum(-1)
        summed = summed * factor[..., None] + jnp.einsum(
            "rhk,kd->rhd",
            weights.astype(jnp.bfloat16),
            values_part,
            preferred_element_type=jnp.float32,
        )
        return (newest, total, summed)

    starting = (
        jnp.full((row_count, heads_here), negative_fill, jnp.float32),
        jnp.zeros((row_count, heads_here), jnp.float32),
        jnp.zeros((row_count, heads_here, HEAD_SIZE), jnp.float32),
    )
    loop_size = lax.axis_size("ctx")
    running = absorb(starting, own_rows, positions)

    def turn(turn_index, state):
        current, rows_now, places_now = state
        rows_now, places_now = shifted((rows_now, places_now), "ctx", 1)
        return (absorb(current, rows_now, places_now), rows_now, places_now)

    running = lax.fori_loop(0, loop_size - 1, turn, (running, own_rows, positions))[0]
    highest, total, summed = running
    attended = (summed / total[..., None]).reshape(row_count, heads_here * HEAD_SIZE)
    return attended.astype(jnp.bfloat16)


def solution(mesh):
    placed = (P("ctx", "head"), P("ctx", None), P("ctx", None), P("ctx"))
    return jax.shard_map(
        body, mesh=mesh, in_specs=placed, out_specs=P("ctx", "head"), check_vma=False
    )
```

profile of v0, /device:TPU:0, one launch (start us, length us, event | category | flops | bytes accessed | tf_op | source)
XLA Modules:
  0.0 35.8 jit_solution(16476495501409452206)
XLA Ops:
  0.0 0.8 %constant_dynamic-slice_fusion = (bf16[192,128]{1,0:T(8,128)(2,1)S(1)}, bf16[192,128]{1,0:T(8,128)(2,1)S(1)}) fusion(bf16[192,1024]{1,0:T(8,128)(2,1)} %param.8, s32[]{:T(128)S(6)} %select_n.23, bf16[192,1024]{1,0:T(8,128)(2,1)} %param.7), kind=kLoop, calls=%fused_computation.38 | loop fusion | bytes 196612 | tf_op jit(solution)/shard_map/dynamic_slice | solution.py:25
  0.8 0.8 %broadcast_compare_fusion.1 = pred[192,192]{0,1:T(8,128)(4,1)S(1)} fusion(s32[192]{0:T(256)} %param.9), kind=kLoop, calls=%fused_computation.33 | loop fusion | flops 36864 | bytes 37632 | tf_op jit(solution)/shard_map/le | solution.py:37
  1.7 1.9 %fusion.16 = (f32[192,16]{0,1:T(8,128)S(1)}, f32[192,192,16]{1,0,2:T(8,128)S(1)}) fusion(pred[192,192]{0,1:T(8,128)(4,1)S(1)} %broadcast_compare_fusion.1, bf16[192,128]{1,0:T(8,128)(2,1)S(1)} %get-tuple-element.85, bf16[192,2048]{1,0:T(8,128)(2,1)} %param.6), kind=kOutput, calls=%fused_computation.23 | convolution fusion | flops 152761344 | bytes 3244032 | tf_op jit(solution)/shard_map/rhd,kd->rhk/dot_general | solution.py:34
  3.6 1.0 %fusion.17 = (bf16[192,16,192]{0,2,1:T(8,128)(2,1)S(1)}, f32[192,16]{0,1:T(8,128)S(1)}) fusion(f32[192,192,16]{1,0,2:T(8,128)S(1)} %get-tuple-element.83, f32[192,16]{0,1:T(8,128)S(1)} %broadcast_maximum_fusion, pred[192,192]{0,1:T(8,128)(4,1)S(1)} %broadcast_compare_fusion.1), kind=kLoop, calls=%fused_computation.24 | loop fusion | flops 3535872 | bytes 3600384 | tf_op jit(solution)/shard_map/convert_element_type | solution.py:45
  4.5 1.5 %copy.10 = bf16[192,16,192]{2,1,0:T(8,128)(2,1)S(1)} copy(bf16[192,16,192]{0,2,1:T(8,128)(2,1)S(1)} %get-tuple-element.78) | data formatting | bytes 2359296 | tf_op jit(solution)/shard_map/convert_element_type | solution.py:45
  6.1 0.0 copy-start
  6.1 0.1 copy.9
  6.2 0.7 %convolution_add_fusion = f32[192,16,128]{2,1,0:T(8,128)S(1)} fusion(bf16[192,16,192]{2,1,0:T(8,128)(2,1)S(1)} %copy.10, f32[192,16]{1,0:T(8,128)S(1)} %copy.9, bf16[192,128]{1,0:T(8,128)(2,1)S(1)} %get-tuple-element.84), kind=kOutput, calls=%fused_computation.27 | convolution fusion | flops 151388160 | bytes 2813952 | tf_op jit(solution)/shard_map/rhk,kd->rhd/dot_general | solution.py:43
  7.0 0.1 copy.12
  7.1 0.1 copy.11
  7.2 1.3 %copy.14 = bf16[24,8,16,128]{3,2,1,0:T(8,128)(2,1)S(1)} copy(bf16[24,8,16,128]{3,1,2,0:T(8,128)(2,1)} %bitcast.51) | data formatting | bytes 1572864
  8.5 0.0 copy-done
  8.5 25.7 %while.18 = (s32[]{:T(128)}, f32[192,16]{1,0:T(8,128)S(1)}, f32[192,16]{1,0:T(8,128)S(1)}, f32[192,16,128]{2,1,0:T(8,128)S(1)}, bf16[192,256]{1,0:T(8,128)(2,1)S...) while((s32[]{:T(128)}, f32[192,16]{1,0:T(8,128)S(1)}, ...), condition=%wide.region_5.6_spmd, body=%wide.region_2.5_spmd.sunk | while | flops 310487040 | bytes 13031597 | solution.py:64
  8.5 0.5 %collective-permute-start = (s32[192]{0:T(256)S(1)}, s32[192]{0:T(256)S(1)}, u32[]{:S(2)}, u32[]{:S(2)}) collective-permute-start(s32[192]{0:T(256)S(1)} %get-tuple-element.157), channel_id=1, source_target_pairs={{3,0},{0,1},{1,2},{2,3},{7,4},{4,5},{5,6},{6,7},{11,8},{8,9},{9,10... | collective-permute-start | bytes 2312 | tf_op jit(solution)/shard_map/while/body/eval_jaxpr/ppermute | solution.py:16
  9.0 2.6 %collective-permute-start.1 = (bf16[192,256]{1,0:T(8,128)(2,1)S(1)}, bf16[192,256]{1,0:T(8,128)(2,1)S(1)}, u32[]{:S(2)}, u32[]{:S(2)}) collective-permute-start(bf16[192,256]{1,0:T(8,128)(2,1)S(1)} %get-tuple-element.156), channel_id=1, source_target_pairs={{3,0},{0,1},{1,2},{2,3},{7,4},{4,5},{5,6},{6,7},{11,8},{8,9},{9,10... | collective-permute-start | bytes 294920 | tf_op jit(solution)/shard_map/while/body/eval_jaxpr/ppermute | solution.py:16
  11.6 0.6 %collective-permute-done = s32[192]{0:T(256)S(1)} collective-permute-done((s32[192]{0:T(256)S(1)}, s32[192]{0:T(256)S(1)}, u32[]{:S(2)}, u32[]{:S(2)}) %collective-permute-start) | collective-permute-done | bytes 800 | tf_op jit(solution)/shard_map/while/body/eval_jaxpr/ppermute | solution.py:16
  12.2 0.1 broadcast_compare_fusion.3
  12.3 1.0 %collective-permute-done.1 = bf16[192,256]{1,0:T(8,128)(2,1)S(1)} collective-permute-done((bf16[192,256]{1,0:T(8,128)(2,1)S(1)}, bf16[192,256]{1,0:T(8,128)(2,1)S(1)}, u32[]{:S(2)}, u32[]{:S(2)}) %collective-permute-start.1) | collective-permute-done | bytes 98336 | tf_op jit(solution)/shard_map/while/body/eval_jaxpr/ppermute | solution.py:16
  13.3 0.8 %fusion.34 = (f32[192,16]{1,0:T(8,128)S(1)}, f32[192,16,192]{2,1,0:T(8,128)S(1)}) fusion(pred[192,192]{1,0:T(8,128)(4,1)S(1)} %broadcast_compare_fusion.3, bf16[192,16,128]{2,1,0:T(8,128)(2,1)S(1)} %get-tuple-element.168, bf16[192,256]{1,0:T(8,128)(2,1)S(1)} %collective-permute-done.1), kind=kOutput, calls=%fused_computation.2.clone.1 | convolution fusion | flops 152761344 | bytes 3256320 | tf_op jit(solution)/shard_map/while/body/eval_jaxpr/rhd,kd->rhk/dot_general | solution.py:34
  14.2 1.6 %fusion.35 = f32[192,16]{1,0:T(8,128)S(1)} fusion(f32[192,16,192]{2,1,0:T(8,128)S(1)} %get-tuple-element.140, f32[192,16]{1,0:T(8,128)S(1)} %max.4, pred[192,192]{1,0:T(8,128)(4,1)S(1)} %broadcast_compare_fusion.3), kind=kLoop, calls=%fused_computation.4.clone.1 | loop fusion | flops 2946048 | bytes 2420736 | tf_op jit(solution)/shard_map/while/body/eval_jaxpr/reduce_sum | solution.py:42
  15.8 0.1 multiply_add_fusion.4
  15.9 1.6 %multiply_add_fusion.5 = f32[192,16,128]{2,1,0:T(8,128)S(1)} fusion(f32[192,16,128]{2,1,0:T(8,128)S(1)} %get-tuple-element.155, f32[192,16,192]{2,1,0:T(8,128)S(1)} %get-tuple-element.140, f32[192,16]{1,0:T(8,128)S(1)} %max.4, pred[192,192]{1,0:T(8,128)(4,1)S(1)} %broadcast_compare_fusion.3, f32[192,16]{1,0:T(8,128)S(1)} %get-tuple-element.142, ...), kind=kOutput, calls=%fused_computation.6.clone.1 | convolution fusion | flops 154730496 | bytes 6586368 | tf_op jit(solution)/shard_map/while/body/eval_jaxpr/rhk,kd->rhd/dot_general | solution.py:43
  17.5 0.1 collective-permute-start
  17.6 2.4 %collective-permute-start.1 = (bf16[192,256]{1,0:T(8,128)(2,1)S(1)}, bf16[192,256]{1,0:T(8,128)(2,1)S(1)}, u32[]{:S(2)}, u32[]{:S(2)}) collective-permute-start(bf16[192,256]{1,0:T(8,128)(2,1)S(1)} %get-tuple-element.156), channel_id=1, source_target_pairs={{3,0},{0,1},{1,2},{2,3},{7,4},{4,5},{5,6},{6,7},{11,8},{8,9},{9,10... | collective-permute-start | bytes 294920 | tf_op jit(solution)/shard_map/while/body/eval_jaxpr/ppermute | solution.py:16
  20.0 0.6 %collective-permute-done = s32[192]{0:T(256)S(1)} collective-permute-done((s32[192]{0:T(256)S(1)}, s32[192]{0:T(256)S(1)}, u32[]{:S(2)}, u32[]{:S(2)}) %collective-permute-start) | collective-permute-done | bytes 800 | tf_op jit(solution)/shard_map/while/body/eval_jaxpr/ppermute | solution.py:16
  20.6 0.1 broadcast_compare_fusion.3
  20.7 1.0 %collective-permute-done.1 = bf16[192,256]{1,0:T(8,128)(2,1)S(1)} collective-permute-done((bf16[192,256]{1,0:T(8,128)(2,1)S(1)}, bf16[192,256]{1,0:T(8,128)(2,1)S(1)}, u32[]{:S(2)}, u32[]{:S(2)}) %collective-permute-start.1) | collective-permute-done | bytes 98336 | tf_op jit(solution)/shard_map/while/body/eval_jaxpr/ppermute | solution.py:16
  21.7 0.8 %fusion.34 = (f32[192,16]{1,0:T(8,128)S(1)}, f32[192,16,192]{2,1,0:T(8,128)S(1)}) fusion(pred[192,192]{1,0:T(8,128)(4,1)S(1)} %broadcast_compare_fusion.3, bf16[192,16,128]{2,1,0:T(8,128)(2,1)S(1)} %get-tuple-element.168, bf16[192,256]{1,0:T(8,128)(2,1)S(1)} %collective-permute-done.1), kind=kOutput, calls=%fused_computation.2.clone.1 | convolution fusion | flops 152761344 | bytes 3256320 | tf_op jit(solution)/shard_map/while/body/eval_jaxpr/rhd,kd->rhk/dot_general | solution.py:34
  22.5 1.6 %fusion.35 = f32[192,16]{1,0:T(8,128)S(1)} fusion(f32[192,16,192]{2,1,0:T(8,128)S(1)} %get-tuple-element.140, f32[192,16]{1,0:T(8,128)S(1)} %max.4, pred[192,192]{1,0:T(8,128)(4,1)S(1)} %broadcast_compare_fusion.3), kind=kLoop, calls=%fused_computation.4.clone.1 | loop fusion | flops 2946048 | bytes 2420736 | tf_op jit(solution)/shard_map/while/body/eval_jaxpr/reduce_sum | solution.py:42
  24.1 0.1 multiply_add_fusion.4
  24.2 1.6 %multiply_add_fusion.5 = f32[192,16,128]{2,1,0:T(8,128)S(1)} fusion(f32[192,16,128]{2,1,0:T(8,128)S(1)} %get-tuple-element.155, f32[192,16,192]{2,1,0:T(8,128)S(1)} %get-tuple-element.140, f32[192,16]{1,0:T(8,128)S(1)} %max.4, pred[192,192]{1,0:T(8,128)(4,1)S(1)} %broadcast_compare_fusion.3, f32[192,16]{1,0:T(8,128)S(1)} %get-tuple-element.142, ...), kind=kOutput, calls=%fused_computation.6.clone.1 | convolution fusion | flops 154730496 | bytes 6586368 | tf_op jit(solution)/shard_map/while/body/eval_jaxpr/rhk,kd->rhd/dot_general | solution.py:43
  25.9 0.1 collective-permute-start
  25.9 2.4 %collective-permute-start.1 = (bf16[192,256]{1,0:T(8,128)(2,1)S(1)}, bf16[192,256]{1,0:T(8,128)(2,1)S(1)}, u32[]{:S(2)}, u32[]{:S(2)}) collective-permute-start(bf16[192,256]{1,0:T(8,128)(2,1)S(1)} %get-tuple-element.156), channel_id=1, source_target_pairs={{3,0},{0,1},{1,2},{2,3},{7,4},{4,5},{5,6},{6,7},{11,8},{8,9},{9,10... | collective-permute-start | bytes 294920 | tf_op jit(solution)/shard_map/while/body/eval_jaxpr/ppermute | solution.py:16
  28.3 0.6 %collective-permute-done = s32[192]{0:T(256)S(1)} collective-permute-done((s32[192]{0:T(256)S(1)}, s32[192]{0:T(256)S(1)}, u32[]{:S(2)}, u32[]{:S(2)}) %collective-permute-start) | collective-permute-done | bytes 800 | tf_op jit(solution)/shard_map/while/body/eval_jaxpr/ppermute | solution.py:16
  28.9 0.1 broadcast_compare_fusion.3
  29.0 1.0 %collective-permute-done.1 = bf16[192,256]{1,0:T(8,128)(2,1)S(1)} collective-permute-done((bf16[192,256]{1,0:T(8,128)(2,1)S(1)}, bf16[192,256]{1,0:T(8,128)(2,1)S(1)}, u32[]{:S(2)}, u32[]{:S(2)}) %collective-permute-start.1) | collective-permute-done | bytes 98336 | tf_op jit(solution)/shard_map/while/body/eval_jaxpr/ppermute | solution.py:16
  30.0 0.8 %fusion.34 = (f32[192,16]{1,0:T(8,128)S(1)}, f32[192,16,192]{2,1,0:T(8,128)S(1)}) fusion(pred[192,192]{1,0:T(8,128)(4,1)S(1)} %broadcast_compare_fusion.3, bf16[192,16,128]{2,1,0:T(8,128)(2,1)S(1)} %get-tuple-element.168, bf16[192,256]{1,0:T(8,128)(2,1)S(1)} %collective-permute-done.1), kind=kOutput, calls=%fused_computation.2.clone.1 | convolution fusion | flops 152761344 | bytes 3256320 | tf_op jit(solution)/shard_map/while/body/eval_jaxpr/rhd,kd->rhk/dot_general | solution.py:34
  30.9 1.6 %fusion.35 = f32[192,16]{1,0:T(8,128)S(1)} fusion(f32[192,16,192]{2,1,0:T(8,128)S(1)} %get-tuple-element.140, f32[192,16]{1,0:T(8,128)S(1)} %max.4, pred[192,192]{1,0:T(8,128)(4,1)S(1)} %broadcast_compare_fusion.3), kind=kLoop, calls=%fused_computation.4.clone.1 | loop fusion | flops 2946048 | bytes 2420736 | tf_op jit(solution)/shard_map/while/body/eval_jaxpr/reduce_sum | solution.py:42
  32.5 0.1 multiply_add_fusion.4
  32.6 1.6 %multiply_add_fusion.5 = f32[192,16,128]{2,1,0:T(8,128)S(1)} fusion(f32[192,16,128]{2,1,0:T(8,128)S(1)} %get-tuple-element.155, f32[192,16,192]{2,1,0:T(8,128)S(1)} %get-tuple-element.140, f32[192,16]{1,0:T(8,128)S(1)} %max.4, pred[192,192]{1,0:T(8,128)(4,1)S(1)} %broadcast_compare_fusion.3, f32[192,16]{1,0:T(8,128)S(1)} %get-tuple-element.142, ...), kind=kOutput, calls=%fused_computation.6.clone.1 | convolution fusion | flops 154730496 | bytes 6586368 | tf_op jit(solution)/shard_map/while/body/eval_jaxpr/rhk,kd->rhd/dot_general | solution.py:43
  34.2 0.5 %divide_convert_fusion = bf16[192,16,128]{2,1,0:T(8,128)(2,1)S(1)} fusion(f32[192,16,128]{2,1,0:T(8,128)S(1)} %get-tuple-element.48, f32[192,16]{1,0:T(8,128)S(1)} %get-tuple-element.49), kind=kLoop, calls=%fused_computation.26 | loop fusion | flops 786432 | bytes 2371584 | tf_op jit(solution)/shard_map/convert_element_type | solution.py:67
  34.7 1.1 %copy.23 = bf16[24,8,16,128]{3,1,2,0:T(8,128)(2,1)} copy(bf16[24,8,16,128]{3,2,1,0:T(8,128)(2,1)S(1)} %bitcast.50) | data formatting | bytes 1572864
  (16 shorter events, 0.1 us)
Async XLA Ops:
  6.1 2.4 %copy-start = (s32[192]{0:T(256)S(1)}, s32[192]{0:T(256)}, u32[]{:S(2)}) copy-start(s32[192]{0:T(256)} %param.9) | copy-start | bytes 2308
  8.5 3.7 %collective-permute-start = (s32[192]{0:T(256)S(1)}, s32[192]{0:T(256)S(1)}, u32[]{:S(2)}, u32[]{:S(2)}) collective-permute-start(s32[192]{0:T(256)S(1)} %get-tuple-element.157), channel_id=1, source_target_pairs={{3,0},{0,1},{1,2},{2,3},{7,4},{4,5},{5,6},{6,7},{11,8},{8,9},{9,10... | collective-permute-start | bytes 2312 | tf_op jit(solution)/shard_map/while/body/eval_jaxpr/ppermute | solution.py:16
  9.0 4.3 %collective-permute-start.1 = (bf16[192,256]{1,0:T(8,128)(2,1)S(1)}, bf16[192,256]{1,0:T(8,128)(2,1)S(1)}, u32[]{:S(2)}, u32[]{:S(2)}) collective-permute-start(bf16[192,256]{1,0:T(8,128)(2,1)S(1)} %get-tuple-element.156), channel_id=1, source_target_pairs={{3,0},{0,1},{1,2},{2,3},{7,4},{4,5},{5,6},{6,7},{11,8},{8,9},{9,10... | collective-permute-start | bytes 294920 | tf_op jit(solution)/shard_map/while/body/eval_jaxpr/ppermute | solution.py:16
  17.5 3.0 %collective-permute-start = (s32[192]{0:T(256)S(1)}, s32[192]{0:T(256)S(1)}, u32[]{:S(2)}, u32[]{:S(2)}) collective-permute-start(s32[192]{0:T(256)S(1)} %get-tuple-element.157), channel_id=1, source_target_pairs={{3,0},{0,1},{1,2},{2,3},{7,4},{4,5},{5,6},{6,7},{11,8},{8,9},{9,10... | collective-permute-start | bytes 2312 | tf_op jit(solution)/shard_map/while/body/eval_jaxpr/ppermute | solution.py:16
  17.6 4.1 %collective-permute-start.1 = (bf16[192,256]{1,0:T(8,128)(2,1)S(1)}, bf16[192,256]{1,0:T(8,128)(2,1)S(1)}, u32[]{:S(2)}, u32[]{:S(2)}) collective-permute-start(bf16[192,256]{1,0:T(8,128)(2,1)S(1)} %get-tuple-element.156), channel_id=1, source_target_pairs={{3,0},{0,1},{1,2},{2,3},{7,4},{4,5},{5,6},{6,7},{11,8},{8,9},{9,10... | collective-permute-start | bytes 294920 | tf_op jit(solution)/shard_map/while/body/eval_jaxpr/ppermute | solution.py:16
  25.9 3.0 %collective-permute-start = (s32[192]{0:T(256)S(1)}, s32[192]{0:T(256)S(1)}, u32[]{:S(2)}, u32[]{:S(2)}) collective-permute-start(s32[192]{0:T(256)S(1)} %get-tuple-element.157), channel_id=1, source_target_pairs={{3,0},{0,1},{1,2},{2,3},{7,4},{4,5},{5,6},{6,7},{11,8},{8,9},{9,10... | collective-permute-start | bytes 2312 | tf_op jit(solution)/shard_map/while/body/eval_jaxpr/ppermute | solution.py:16
  25.9 4.1 %collective-permute-start.1 = (bf16[192,256]{1,0:T(8,128)(2,1)S(1)}, bf16[192,256]{1,0:T(8,128)(2,1)S(1)}, u32[]{:S(2)}, u32[]{:S(2)}) collective-permute-start(bf16[192,256]{1,0:T(8,128)(2,1)S(1)} %get-tuple-element.156), channel_id=1, source_target_pairs={{3,0},{0,1},{1,2},{2,3},{7,4},{4,5},{5,6},{6,7},{11,8},{8,9},{9,10... | collective-permute-start | bytes 294920 | tf_op jit(solution)/shard_map/while/body/eval_jaxpr/ppermute | solution.py:16
where the time goes:
time: 36 us; the launch traced here: 35.8 us
  matrix products  9.9 us (28%)
  starting transfers between devices  8.03 us (22%)
  other arithmetic  7.6 us (21%)
  local copies, waits for them, and re-layouts  5.11 us (14%)
  waiting for transfers between devices  4.77 us (13%)
    ppermute x6, starting transfers between devices, shifted(): return lax.ppermute(block, axis, route)  8.03 us
    dot_general x4, matrix products, absorb(): jnp.einsum('rhk,kd->rhd', weights.astype(jnp.bfloat16), values_part, pref...  5.54 us
    ppermute x6, waiting for transfers between devices, shifted(): return lax.ppermute(block, axis, route)  4.77 us
    reduce_sum x3, other arithmetic, absorb(): total = total * factor + weights.sum(-1)  4.76 us
    dot_general x4, matrix products, absorb(): jnp.einsum('rhd,kd->rhk', query_view, keys_part, preferred_element_type=j...  4.35 us
    unnamed x5, local copies, waits for them, and re-layouts  2.38 us
    convert_element_type x1, local copies, waits for them, and re-layouts, absorb(): weights.astype(jnp.bfloat16)  1.54 us
    le x4, other arithmetic, absorb(): allowed = (key_positions[None, :] <= positions[:, None])[:, None, :]  1.13 us
  transfers between devices with their start and end apart: 6, of which 6 were waited for; matrix products, arithmetic and copies ran while one was open for 1% of the time, Pallas kernels for 0%

commit v1 on v0

v1 whole, which is shorter than its diff:
```python
import functools

import jax
import jax.numpy as jnp
from jax import lax
from jax.experimental import pallas as pl
from jax.experimental.pallas import tpu as pltpu
from jax.sharding import PartitionSpec as P

HEAD_SIZE = 128
QUERIES_PER_KV = 16
SPAN = 96
SCALE = HEAD_SIZE ** (-0.5)
SCALE_TWO = SCALE * 1.4426950408889634
ONES_ROWS = 16
negative_fill = -1e30
LEAST_TOTAL = 1e-25
LARGEST_TOTAL = 1e25

f32 = jnp.float32
bf16 = jnp.bfloat16


def nt(a, b):
    return lax.dot_general(a, b, (((1,), (1,)), ((), ())), preferred_element_type=f32)


def attention(group_blocks, positions_ref, q_ref, *refs):
    *payloads, out_ref, keys_ref, values_ref, spans_ref, acc_ref = refs
    rows = q_ref.shape[0]
    heads = q_ref.shape[1] // HEAD_SIZE
    spans = rows // SPAN
    block = rows + ONES_ROWS
    blocks = [(ref, i) for ref in payloads for i in range(ref.shape[0] // block)]
    keys = len(blocks) * rows
    width = heads * SPAN
    group = group_blocks * rows
    groups = keys // group

    for at, (ref, i) in enumerate(blocks):
        top, here = i * block, slice(at * rows, (at + 1) * rows)
        keys_ref[here, :] = ref[top : top + rows, :HEAD_SIZE]
        values_ref[:HEAD_SIZE, here] = ref[top : top + rows, HEAD_SIZE:].T
        spans_ref[:, here] = jnp.broadcast_to(ref[top + rows : top + rows + 1, :rows], (ONES_ROWS, rows))
    values_ref[HEAD_SIZE:, :] = jnp.ones((ONES_ROWS, keys), bf16)

    def triangle(columns):
        key = lax.broadcasted_iota(jnp.int32, (SPAN, columns), 0)
        query = lax.broadcasted_iota(jnp.int32, (SPAN, columns), 1) % SPAN
        return key <= query

    fine = None
    for s in range(spans):
        here = slice(s * SPAN, (s + 1) * SPAN)
        span = (positions_ref[s * SPAN] // SPAN).astype(f32)
        q = jnp.concatenate(
            [q_ref[here, h * HEAD_SIZE : (h + 1) * HEAD_SIZE] for h in range(heads)], 0
        )

        def part(first, own):
            allowed = (spans_ref[:, pl.ds(first, group)].astype(f32) <= span).astype(f32).astype(bf16)
            values = values_ref[:, pl.ds(first, group)] * allowed[:1]
            weights = jnp.exp2(nt(keys_ref[pl.ds(first, group), :], q) * SCALE_TWO)
            if own:
                diagonal = jnp.where(triangle(width), weights[here], 0.0)
                pieces = [weights[: s * SPAN], diagonal, weights[(s + 1) * SPAN :]]
                weights = jnp.concatenate([p for p in pieces if p.shape[0]], 0)
            return jnp.dot(values, weights.astype(bf16), preferred_element_type=f32)

        summed = part(0, True)
        if groups > 1:
            acc_ref[...] = summed

            @pl.loop(1, groups)
            def _(g):
                acc_ref[...] += part(pl.multiple_of(g * group, group), False)

            summed = acc_ref[...]
        total = summed[HEAD_SIZE : HEAD_SIZE + 1]
        inside = jnp.where((total >= LEAST_TOTAL) & (total <= LARGEST_TOTAL), 1.0, 0.0)
        fine = inside if fine is None else jnp.minimum(fine, inside)
        attended = (summed[:HEAD_SIZE] / total).T.astype(bf16)
        for h in range(heads):
            out_ref[here, h * HEAD_SIZE : (h + 1) * HEAD_SIZE] = attended[h * SPAN : (h + 1) * SPAN]

    @pl.when(jnp.min(fine) < 0.5)
    def _():
        def head(h, carry):
            at = pl.ds(pl.multiple_of(h * HEAD_SIZE, HEAD_SIZE), HEAD_SIZE)
            for s in range(spans):
                here = slice(s * SPAN, (s + 1) * SPAN)
                span = (positions_ref[s * SPAN] // SPAN).astype(f32)
                q = q_ref[here, at]

                def part(g, state):
                    highest, summed = state
                    first = pl.multiple_of(g * group, group)
                    place = spans_ref[:1, pl.ds(first, group)].astype(f32)
                    column = jnp.broadcast_to(place, (HEAD_SIZE, group)).T[:, :SPAN]
                    key = lax.broadcasted_iota(jnp.int32, (group, SPAN), 0) + first
                    query = lax.broadcasted_iota(jnp.int32, (group, SPAN), 1) + s * SPAN
                    later = (key >= s * SPAN) & (key < (s + 1) * SPAN) & (key > query)
                    allowed = (column <= span) & jnp.logical_not(later)
                    scores = nt(keys_ref[pl.ds(first, group), :], q) * SCALE
                    scores = jnp.where(allowed, scores, negative_fill)
                    newest = jnp.maximum(highest, jnp.max(scores, 0, keepdims=True))
                    weights = jnp.where(allowed, jnp.exp(scores - newest), 0.0).astype(bf16)
                    summed = summed * jnp.exp(highest - newest) + jnp.dot(
                        values_ref[:, pl.ds(first, group)], weights, preferred_element_type=f32
                    )
                    return newest, summed

                state = (
                    jnp.full((1, SPAN), negative_fill, f32),
                    jnp.zeros((HEAD_SIZE + ONES_ROWS, SPAN), f32),
                )
                summed = lax.fori_loop(0, groups, part, state)[1]
                out_ref[here, at] = (summed[:HEAD_SIZE] / summed[HEAD_SIZE : HEAD_SIZE + 1]).T.astype(bf16)
            return carry

        lax.fori_loop(0, heads, head, 0)


def attend(queries, positions, payloads, group_blocks):
    rows = queries.shape[0]
    heads = queries.shape[1] // HEAD_SIZE
    keys = sum(p.shape[0] for p in payloads) // (rows + ONES_ROWS) * rows
    vmem = pl.BlockSpec(memory_space=pltpu.VMEM)
    return pl.pallas_call(
        functools.partial(attention, group_blocks),
        out_shape=jax.ShapeDtypeStruct(queries.shape, bf16),
        in_specs=[pl.BlockSpec(memory_space=pltpu.SMEM)] + [vmem] * (1 + len(payloads)),
        out_specs=vmem,
        scratch_shapes=[
            pltpu.VMEM((keys, HEAD_SIZE), bf16),
            pltpu.VMEM((HEAD_SIZE + ONES_ROWS, keys), bf16),
            pltpu.VMEM((ONES_ROWS, keys), bf16),
            pltpu.VMEM((HEAD_SIZE + ONES_ROWS, heads * SPAN), f32),
        ],
        compiler_params=pltpu.CompilerParams(vmem_limit_bytes=40 << 20),
    )(positions, queries, *payloads)


def swapped(block, bit):
    devices = range(lax.axis_size("ctx"))
    return lax.ppermute(block, "ctx", [(i ^ bit, i) for i in devices])


def body(queries, rotated_key_rows, value_state_rows, positions):
    row_count = queries.shape[0]
    heads_here = queries.shape[1] // HEAD_SIZE
    group_index = lax.axis_index("head") * heads_here // QUERIES_PER_KV
    key_slice = lax.dynamic_slice_in_dim(rotated_key_rows, group_index * HEAD_SIZE, HEAD_SIZE, 1)
    value_slice = lax.dynamic_slice_in_dim(value_state_rows, group_index * HEAD_SIZE, HEAD_SIZE, 1)
    own_rows = jnp.concatenate([key_slice, value_slice], 1)
    spans = jnp.pad((positions // SPAN).astype(bf16)[None], ((0, ONES_ROWS - 1), (0, 2 * HEAD_SIZE - row_count)))
    own = jnp.concatenate([own_rows, spans], 0)
    if lax.axis_size("ctx") == 4:
        core = swapped(own, 1)
        chip = swapped(own, 2)
        both = swapped(chip, 1)
        payloads = [own, core, chip, both]
    else:
        size = lax.axis_size("ctx")
        everyone = lax.all_gather(own, "ctx", axis=0)
        others = (lax.axis_index("ctx") + jnp.arange(size)) % size
        payloads = [jnp.take(everyone, others, axis=0).reshape(-1, 2 * HEAD_SIZE)]
    return attend(queries, positions, payloads, 4)


def solution(mesh):
    placed = (P("ctx", "head"), P("ctx", None), P("ctx", None), P("ctx"))
    return jax.shard_map(
        body, mesh=mesh, in_specs=placed, out_specs=P("ctx", "head"), check_vma=False
    )
```

time: 36 us -> 27.2 us (0.76)
  Pallas kernels: 0 us -> 17 us
  matrix products: 9.9 us -> 0 us
  other arithmetic: 7.6 us -> 0.03 us
  starting transfers between devices: 8.03 us -> 3.04 us
  local copies, waits for them, and re-layouts: 5.11 us -> 2.66 us
  waiting for transfers between devices: 4.77 us -> 4.28 us
    pallas_call x0 -> x1, Pallas kernels: none -> 17 us  [attend(): pl.pallas_call(functools.partial(attention, group_blocks), out_shape=jax....]
    dot_general x8 -> x0, matrix products: 9.9 us -> none  [the longest x4 5.54 us: absorb(): jnp.einsum('rhk,kd->rhd', weights.astype(jnp.bfloat16), values_part, pref...]
    ppermute x6 -> x3, starting transfers between devices: 8.03 us -> 3.04 us  [swapped(): return lax.ppermute(block, 'ctx', [(i ^ bit, i) for i in devices])]
    reduce_sum x3 -> x0, other arithmetic: 4.76 us -> none  [absorb(): total = total * factor + weights.sum(-1)]
    convert_element_type x1 -> x0, local copies, waits for them, and re-layouts: 1.54 us -> none  [absorb(): weights.astype(jnp.bfloat16)]
    convert_element_type x2 -> x1, other arithmetic: 1.44 us -> 0.01 us  [body(): (positions // SPAN).astype(bf16)[None]]
    le x4 -> x0, other arithmetic: 1.13 us -> none  [absorb(): allowed = (key_positions[None, :] <= positions[:, None])[:, None, :]]
    unnamed x5 -> x4, local copies, waits for them, and re-layouts: 2.38 us -> 1.81 us
  transfers between devices with their start and end apart: 6 -> 3, of which waited for: 6 -> 2; matrix products, arithmetic and copies ran while one was open for 1% -> 0% of each run, Pallas kernels for 0% -> 0%
where the time goes in v1:
time: 27.2 us; the launch traced here: 27 us
  Pallas kernels  17 us (62%)
  waiting for transfers between devices  4.28 us (16%)
  starting transfers between devices  3.04 us (11%)
  local copies, waits for them, and re-layouts  2.66 us (10%)
    pallas_call x1, Pallas kernels, attend(): pl.pallas_call(functools.partial(attention, group_blocks), out_shape=jax....  17 us
    ppermute x3, waiting for transfers between devices, swapped(): return lax.ppermute(block, 'ctx', [(i ^ bit, i) for i in devices])  4.28 us
    ppermute x3, starting transfers between devices, swapped(): return lax.ppermute(block, 'ctx', [(i ^ bit, i) for i in devices])  3.04 us
    unnamed x4, local copies, waits for them, and re-layouts  1.81 us
    dynamic_slice x1, local copies, waits for them, and re-layouts, body(): lax.dynamic_slice_in_dim(value_state_rows, group_index * HEAD_SIZE, HEAD_...  0.84 us
  transfers between devices with their start and end apart: 3, of which 2 were waited for; matrix products, arithmetic and copies ran while one was open for 0% of the time, Pallas kernels for 0%

profile of v1, /device:TPU:0, one launch (start us, length us, event | category | flops | bytes accessed | tf_op | source)
XLA Modules:
  0.0 27.0 jit_solution(2629660400890494479)
XLA Ops:
  0.0 0.0 copy-start.1
  0.0 0.7 %copy-done.1 = s32[192]{0:T(256)S(1)} copy-done((s32[192]{0:T(256)S(1)}, s32[192]{0:T(256)}, u32[]{:S(2)}) %copy-start.1) | copy-done | bytes 792
  0.7 0.8 %constant_dynamic-slice_fusion = (bf16[192,128]{1,0:T(8,128)(2,1)S(1)}, bf16[192,128]{1,0:T(8,128)(2,1)S(1)}) fusion(bf16[192,1024]{1,0:T(8,128)(2,1)} %param.6, s32[]{:T(128)S(6)} %select_n.15, bf16[192,1024]{1,0:T(8,128)(2,1)} %param.5), kind=kLoop, calls=%fused_computation.5 | loop fusion | bytes 196612 | tf_op jit(solution)/shard_map/dynamic_slice | solution.py:154
  1.6 3.0 %collective-permute-start.1 = (bf16[208,256]{1,0:T(8,128)(2,1)S(1)}, bf16[208,256]{1,0:T(8,128)(2,1)S(1)}, u32[]{:S(2)}, u32[]{:S(2)}) collective-permute-start(bf16[208,256]{1,0:T(8,128)(2,1)S(1)} %fusion.1.refs_0_), channel_id=1, source_target_pairs={{2,0},{3,1},{0,2},{1,3},{6,4},{7,5},{4,6},{5,7},{10,8},{11,9},{8,1... | collective-permute-start | bytes 319496 | tf_op jit(solution)/shard_map/ppermute | solution.py:146
  4.6 0.0 collective-permute-start
  4.6 3.0 %collective-permute-done.1.refs_2_ = bf16[208,256]{1,0:T(8,128)(2,1)S(1)} collective-permute-done((bf16[208,256]{1,0:T(8,128)(2,1)S(1)}, bf16[208,256]{1,0:T(8,128)(2,1)S(1)}, u32[]{:S(2)}, u32[]{:S(2)}) %collective-permute-start.1) | collective-permute-done | bytes 106528 | tf_op jit(solution)/shard_map/ppermute | solution.py:146
  7.6 0.0 collective-permute-start.2
  7.6 0.0 collective-permute-done.refs_1_
  7.6 1.3 %collective-permute-done.2.refs_3_ = bf16[208,256]{1,0:T(8,128)(2,1)S(1)} collective-permute-done((bf16[208,256]{1,0:T(8,128)(2,1)S(1)}, bf16[208,256]{1,0:T(8,128)(2,1)S(1)}, u32[]{:S(2)}, u32[]{:S(2)}) %collective-permute-start.2) | collective-permute-done | bytes 106528 | tf_op jit(solution)/shard_map/ppermute | solution.py:146
  8.9 0.0 copy-start
  8.9 1.1 %copy-done = bf16[192,2048]{1,0:T(8,128)(2,1)S(1)} copy-done((bf16[192,2048]{1,0:T(8,128)(2,1)S(1)}, bf16[192,2048]{1,0:T(8,128)(2,1)}, u32[]{:S(2)}) %copy-start) | copy-done | bytes 786456
  10.0 17.0 %shard_map.46 = bf16[192,2048]{1,0:T(8,128)(2,1)} custom-call(s32[192]{0:T(256)S(1)} %copy-done.1, bf16[192,2048]{1,0:T(8,128)(2,1)S(1)} %copy-done, bf16[208,256]{1,0:T(8,128)(2,1)S(1)} %fusion.1.refs_0_, bf16[208,256]{1,0:T(8,128)(2,1)S(1)} %collective-permute-done.refs_1_, bf16[208,256]{1,0:T(8,128)(2,1)S(1)} %collective-permute-done.1.refs_2_, ...), custom_call_target="tpu_custom_call" | custom-call | tf_op jit(solution)/shard_map/pallas_call | solution.py:129
  (3 shorter events, 0.0 us)
Async XLA Ops:
  0.0 0.7 %copy-start.1 = (s32[192]{0:T(256)S(1)}, s32[192]{0:T(256)}, u32[]{:S(2)}) copy-start(s32[192]{0:T(256)} %positions_ref.1) | copy-start | bytes 2308
  1.6 6.0 %collective-permute-start.1 = (bf16[208,256]{1,0:T(8,128)(2,1)S(1)}, bf16[208,256]{1,0:T(8,128)(2,1)S(1)}, u32[]{:S(2)}, u32[]{:S(2)}) collective-permute-start(bf16[208,256]{1,0:T(8,128)(2,1)S(1)} %fusion.1.refs_0_), channel_id=1, source_target_pairs={{2,0},{3,1},{0,2},{1,3},{6,4},{7,5},{4,6},{5,7},{10,8},{11,9},{8,1... | collective-permute-start | bytes 319496 | tf_op jit(solution)/shard_map/ppermute | solution.py:146
  4.6 3.0 %collective-permute-start = (bf16[208,256]{1,0:T(8,128)(2,1)S(1)}, bf16[208,256]{1,0:T(8,128)(2,1)S(1)}, u32[]{:S(2)}, u32[]{:S(2)}) collective-permute-start(bf16[208,256]{1,0:T(8,128)(2,1)S(1)} %fusion.1.refs_0_), channel_id=1, source_target_pairs={{1,0},{0,1},{3,2},{2,3},{5,4},{4,5},{7,6},{6,7},{9,8},{8,9},{11,10... | collective-permute-start | bytes 319496 | tf_op jit(solution)/shard_map/ppermute | solution.py:146
  7.6 1.3 %collective-permute-start.2 = (bf16[208,256]{1,0:T(8,128)(2,1)S(1)}, bf16[208,256]{1,0:T(8,128)(2,1)S(1)}, u32[]{:S(2)}, u32[]{:S(2)}) collective-permute-start(bf16[208,256]{1,0:T(8,128)(2,1)S(1)} %collective-permute-done.1.refs_2_), channel_id=1, source_target_pairs={{1,0},{0,1},{3,2},{2,3},{5,4},{4,5},{7,6},{6,7},{9,8},{8,9},{11,10... | collective-permute-start | bytes 319496 | tf_op jit(solution)/shard_map/ppermute | solution.py:146
  8.9 1.1 %copy-start = (bf16[192,2048]{1,0:T(8,128)(2,1)S(1)}, bf16[192,2048]{1,0:T(8,128)(2,1)}, u32[]{:S(2)}) copy-start(bf16[192,2048]{1,0:T(8,128)(2,1)} %q_ref.1) | copy-start | bytes 2359300

commit v2 on v1

v2 whole, which is shorter than its diff:
```python
import functools

import jax
import jax.numpy as jnp
from jax import lax
from jax.experimental import pallas as pl
from jax.experimental.pallas import tpu as pltpu
from jax.sharding import PartitionSpec as P

HEAD_SIZE = 128
QUERIES_PER_KV = 16
SPAN = 96
SCALE = HEAD_SIZE ** (-0.5)
SCALE_TWO = SCALE * 1.4426950408889634
TAIL = 16
SUMS = HEAD_SIZE + TAIL
negative_fill = -1e30
LEAST_TOTAL = 1e-25
LARGEST_TOTAL = 1e25
VMEM_LIMIT = 40 << 20

f32 = jnp.float32
bf16 = jnp.bfloat16
in_vmem = pl.BlockSpec(memory_space=pltpu.VMEM)
in_hbm = pl.BlockSpec(memory_space=pltpu.HBM)


def nt(a, b):
    return lax.dot_general(a, b, (((1,), (1,)), ((), ())), preferred_element_type=f32)


def pack(keys, values, positions, heads):
    rows = keys.shape[0]
    group = lax.axis_index("head") * heads // QUERIES_PER_KV
    ours = [lax.dynamic_slice_in_dim(a, group * HEAD_SIZE, HEAD_SIZE, 1) for a in (keys, values)]
    *ours, positions = lax.optimization_barrier((*ours, positions))
    places = (positions // SPAN).astype(bf16)[None]
    places = jnp.pad(places, ((0, TAIL - 1), (0, 2 * HEAD_SIZE - rows)))
    return jnp.concatenate([jnp.concatenate(ours, 1), places], 0)


def blocks_of(payloads, rows):
    return [
        (ref, i * (rows + TAIL)) for ref in payloads for i in range(ref.shape[0] // (rows + TAIL))
    ]


def unpack(payloads, rows, keys_ref, values_ref, spans_ref):
    for at, (ref, top) in enumerate(blocks_of(payloads, rows)):
        here = slice(at * rows, (at + 1) * rows)
        keys_ref[here, :] = ref[top : top + rows, :HEAD_SIZE]
        values_ref[:HEAD_SIZE, here] = ref[top : top + rows, HEAD_SIZE:].T
        spans_ref[:, here] = ref[top + rows : top + rows + TAIL, :rows]
    values_ref[HEAD_SIZE:, :] = jnp.ones((TAIL, values_ref.shape[1]), bf16)


def stacked(q_ref, s, heads):
    here = slice(s * SPAN, (s + 1) * SPAN)
    return jnp.concatenate(
        [q_ref[here, h * HEAD_SIZE : (h + 1) * HEAD_SIZE] for h in range(heads)], 0
    )


def part(q, span, first, count, keys_ref, values_ref, spans_ref, own=None):
    some = pl.ds(first, count)
    allowed = (spans_ref[:1, some].astype(f32) <= span).astype(f32).astype(bf16)
    values = values_ref[:, some] * allowed
    weights = jnp.exp2(nt(keys_ref[some, :], q) * SCALE_TWO)
    if own is not None:
        key = lax.broadcasted_iota(jnp.int32, (SPAN, q.shape[0]), 0)
        query = lax.broadcasted_iota(jnp.int32, (SPAN, q.shape[0]), 1) % SPAN
        low, high = own * SPAN, (own + 1) * SPAN
        pieces = [weights[:low], jnp.where(key <= query, weights[low:high], 0.0), weights[high:]]
        weights = jnp.concatenate([p for p in pieces if p.shape[0]], 0)
    return jnp.dot(values, weights.astype(bf16), preferred_element_type=f32)


def first_kernel(queries_ref, *refs):
    *payloads, sums_ref, q_ref, keys_ref, values_ref, spans_ref, sems = refs
    rows = q_ref.shape[0]
    heads = q_ref.shape[1] // HEAD_SIZE
    copies = []
    for s in range(rows // SPAN):
        here = pl.ds(s * SPAN, SPAN)
        copies.append(pltpu.make_async_copy(queries_ref.at[here, :], q_ref.at[here, :], sems.at[s]))
        copies[-1].start()
    unpack(payloads, rows, keys_ref, values_ref, spans_ref)
    for s in range(rows // SPAN):
        copies[s].wait()
        span = spans_ref[:1, s * SPAN : s * SPAN + 1].astype(f32)
        sums_ref[s] = part(
            stacked(q_ref, s, heads), span, 0, keys_ref.shape[0], keys_ref, values_ref, spans_ref, s
        )


def first_part(queries, payloads):
    rows = queries.shape[0]
    heads = queries.shape[1] // HEAD_SIZE
    keys = sum(p.shape[0] for p in payloads) // (rows + TAIL) * rows
    return pl.pallas_call(
        first_kernel,
        out_shape=(
            jax.ShapeDtypeStruct((rows // SPAN, SUMS, heads * SPAN), f32),
            jax.ShapeDtypeStruct(queries.shape, bf16),
        ),
        in_specs=[in_hbm] + [in_vmem] * len(payloads),
        out_specs=(in_vmem, in_vmem),
        scratch_shapes=[
            pltpu.VMEM((keys, HEAD_SIZE), bf16),
            pltpu.VMEM((SUMS, keys), bf16),
            pltpu.VMEM((TAIL, keys), bf16),
            pltpu.SemaphoreType.DMA((rows // SPAN,)),
        ],
        compiler_params=pltpu.CompilerParams(vmem_limit_bytes=VMEM_LIMIT),
        cost_estimate=pl.CostEstimate(
            flops=4 * rows * heads * keys * HEAD_SIZE,
            bytes_accessed=4 * rows * heads * HEAD_SIZE,
            transcendentals=rows * heads * keys,
        ),
    )(queries, *payloads)


def last_kernel(held, group, sums_ref, q_ref, *refs):
    *payloads, out_ref, keys_ref, values_ref, spans_ref, acc_ref, ready_ref, sems = refs
    rows = q_ref.shape[0]
    heads = q_ref.shape[1] // HEAD_SIZE
    spans = rows // SPAN
    own = payloads[0]
    unpack(payloads[held:], rows, keys_ref, values_ref, spans_ref)
    groups = keys_ref.shape[0] // group

    def copy(s):
        here = pl.ds(s * SPAN, SPAN)
        return pltpu.make_async_copy(ready_ref.at[here, :], out_ref.at[here, :], sems.at[s])

    fine = None
    for s in range(spans):
        here = slice(s * SPAN, (s + 1) * SPAN)
        span = own[rows : rows + 1, s * SPAN : s * SPAN + 1].astype(f32)
        q = stacked(q_ref, s, heads)
        summed = sums_ref[s] + part(q, span, 0, group, keys_ref, values_ref, spans_ref)
        if groups > 1:
            acc_ref[...] = summed

            @pl.loop(1, groups)
            def _(g):
                first = pl.multiple_of(g * group, group)
                acc_ref[...] += part(q, span, first, group, keys_ref, values_ref, spans_ref)

            summed = acc_ref[...]
        total = summed[HEAD_SIZE : HEAD_SIZE + 1]
        inside = jnp.where((total >= LEAST_TOTAL) & (total <= LARGEST_TOTAL), 1.0, 0.0)
        fine = inside if fine is None else jnp.minimum(fine, inside)
        attended = (summed[:HEAD_SIZE] * (1.0 / total)).T.astype(bf16)
        for h in range(heads):
            ready_ref[here, h * HEAD_SIZE : (h + 1) * HEAD_SIZE] = attended[h * SPAN : (h + 1) * SPAN]
        copy(s).start()
    for s in range(spans):
        copy(s).wait()

    @pl.when(jnp.min(fine) < 0.5)
    def _():
        @pl.loop(0, heads)
        def _(h):
            at = pl.ds(pl.multiple_of(h * HEAD_SIZE, HEAD_SIZE), HEAD_SIZE)
            for s in range(spans):
                careful(payloads, q_ref, ready_ref, s, at)

        for s in range(spans):
            copy(s).start()
        for s in range(spans):
            copy(s).wait()


def careful(payloads, q_ref, ready_ref, s, at):
    rows = q_ref.shape[0]
    own = payloads[0]
    here = slice(s * SPAN, (s + 1) * SPAN)
    span = own[rows : rows + 1, s * SPAN : s * SPAN + 1].astype(f32)
    q = q_ref[here, at]

    def absorb(ref, top, diagonal, state):
        highest, total, summed = state
        keys = ref[pl.ds(top, rows), :HEAD_SIZE]
        values = ref[pl.ds(top, rows), HEAD_SIZE:]
        place = ref[pl.ds(top + rows, TAIL), :][:1].astype(f32)
        column = jnp.broadcast_to(place, (HEAD_SIZE, 2 * HEAD_SIZE)).T[:rows, :SPAN]
        allowed = column <= span
        if diagonal:
            key = lax.broadcasted_iota(jnp.int32, (rows, SPAN), 0)
            query = lax.broadcasted_iota(jnp.int32, (rows, SPAN), 1) + s * SPAN
            later = (key >= s * SPAN) & (key < (s + 1) * SPAN) & (key > query)
            allowed = allowed & jnp.logical_not(later)
        scores = jnp.where(allowed, nt(keys, q) * SCALE, negative_fill)
        newest = jnp.maximum(highest, jnp.max(scores, 0, keepdims=True))
        weights = jnp.where(allowed, jnp.exp(scores - newest), 0.0)
        factor = jnp.exp(highest - newest)
        total = total * factor + jnp.sum(weights, 0, keepdims=True)
        summed = summed * factor + jnp.dot(values.T, weights.astype(bf16), preferred_element_type=f32)
        return newest, total, summed

    state = (
        jnp.full((1, SPAN), negative_fill, f32),
        jnp.zeros((1, SPAN), f32),
        jnp.zeros((HEAD_SIZE, SPAN), f32),
    )
    for ref in payloads:
        if ref is own:
            state = absorb(ref, 0, True, state)
        else:
            block = rows + TAIL
            state = lax.fori_loop(
                0,
                ref.shape[0] // block,
                lambda i, state: absorb(ref, pl.multiple_of(i * block, TAIL), False, state),
                state,
            )
    ready_ref[here, at] = (state[2] / state[1]).T.astype(bf16)


def last_part(sums, queries, payloads, held, group_blocks):
    rows = queries.shape[0]
    heads = queries.shape[1] // HEAD_SIZE
    keys = sum(p.shape[0] for p in payloads[held:]) // (rows + TAIL) * rows
    return pl.pallas_call(
        functools.partial(last_kernel, held, group_blocks * rows),
        out_shape=jax.ShapeDtypeStruct(queries.shape, bf16),
        in_specs=[in_vmem] * (2 + len(payloads)),
        out_specs=in_hbm,
        scratch_shapes=[
            pltpu.VMEM((keys, HEAD_SIZE), bf16),
            pltpu.VMEM((SUMS, keys), bf16),
            pltpu.VMEM((TAIL, keys), bf16),
            pltpu.VMEM((SUMS, heads * SPAN) if keys > group_blocks * rows else (8, HEAD_SIZE), f32),
            pltpu.VMEM(queries.shape, bf16),
            pltpu.SemaphoreType.DMA((rows // SPAN,)),
        ],
        compiler_params=pltpu.CompilerParams(vmem_limit_bytes=VMEM_LIMIT),
        cost_estimate=pl.CostEstimate(
            flops=4 * rows * heads * keys * HEAD_SIZE,
            bytes_accessed=2 * rows * heads * HEAD_SIZE,
            transcendentals=rows * heads * keys,
        ),
    )(sums, queries, *payloads)


def swapped(block, bit):
    devices = range(lax.axis_size("ctx"))
    return lax.ppermute(block, "ctx", [(i ^ bit, i) for i in devices])


def body(queries, rotated_key_rows, value_state_rows, positions):
    heads_here = queries.shape[1] // HEAD_SIZE
    own = pack(rotated_key_rows, value_state_rows, positions, heads_here)
    size = lax.axis_size("ctx")
    if size == 4:
        core = swapped(own, 1)
        chip = swapped(own, 2)
        sums, q = first_part(queries, [own, core])
        chip, sums = lax.optimization_barrier((chip, sums))
        both = swapped(chip, 1)
        return last_part(sums, q, [own, core, chip, both], 2, 2)
    everyone = lax.all_gather(own, "ctx", axis=0)
    others = (lax.axis_index("ctx") + jnp.arange(1, size)) % size
    others = jnp.take(everyone, others, axis=0)
    rest = others[1:].reshape(-1, 2 * HEAD_SIZE)
    sums, q = first_part(queries, [own, others[0]])
    return last_part(sums, q, [own, others[0], rest], 2, 2)


def solution(mesh):
    placed = (P("ctx", "head"), P("ctx", None), P("ctx", None), P("ctx"))
    return jax.shard_map(
        body, mesh=mesh, in_specs=placed, out_specs=P("ctx", "head"), check_vma=False
    )
```

time: 27.2 us -> 30.3 us (1.11)
  Pallas kernels: 17 us -> 22.6 us
  waiting for transfers between devices: 4.28 us -> 1.67 us
  local copies, waits for them, and re-layouts: 2.66 us -> 1.97 us
  other arithmetic: 0.03 us -> 0.71 us
    pallas_call x1 -> x2, Pallas kernels: 17 us -> 22.6 us  [the longest x1 20.5 us: last_part(): pl.pallas_call(functools.partial(last_kernel, held, group_blocks * rows),...]
    ppermute x3, waiting for transfers between devices: 4.28 us -> 1.67 us  [swapped(): return lax.ppermute(block, 'ctx', [(i ^ bit, i) for i in devices])]
    unnamed x4 -> x2, local copies, waits for them, and re-layouts: 1.81 us -> 1.13 us
    convert_element_type x1, other arithmetic: 0.01 us -> 0.69 us  [pack(): places = (positions // SPAN).astype(bf16)[None]]
  transfers between devices with their start and end apart: 3 -> 3, of which waited for: 2 -> 2; matrix products, arithmetic and copies ran while one was open for 0% -> 0% of each run, Pallas kernels for 0% -> 7%
where the time goes in v2:
time: 30.3 us; the launch traced here: 30.1 us
  Pallas kernels  22.6 us (75%)
  starting transfers between devices  3.11 us (10%)
  local copies, waits for them, and re-layouts  1.97 us (7%)
  waiting for transfers between devices  1.67 us (6%)
  other arithmetic  0.71 us (2%)
    pallas_call x1, Pallas kernels, last_part(): pl.pallas_call(functools.partial(last_kernel, held, group_blocks * rows),...  20.5 us
    ppermute x3, starting transfers between devices, swapped(): return lax.ppermute(block, 'ctx', [(i ^ bit, i) for i in devices])  3.11 us
    pallas_call x1, Pallas kernels, first_part(): pl.pallas_call(first_kernel, out_shape=(jax.ShapeDtypeStruct((rows // SPA...  2.06 us
    ppermute x3, waiting for transfers between devices, swapped(): return lax.ppermute(block, 'ctx', [(i ^ bit, i) for i in devices])  1.67 us
    unnamed x2, local copies, waits for them, and re-layouts  1.13 us
    dynamic_slice x1, local copies, waits for them, and re-layouts, pack(): lax.dynamic_slice_in_dim(a, group * HEAD_SIZE, HEAD_SIZE, 1)  0.83 us
    convert_element_type x1, other arithmetic, pack(): places = (positions // SPAN).astype(bf16)[None]  0.69 us
  transfers between devices with their start and end apart: 3, of which 2 were waited for; matrix products, arithmetic and copies ran while one was open for 0% of the time, Pallas kernels for 7%

profile of v2, /device:TPU:0, one launch (start us, length us, event | category | flops | bytes accessed | tf_op | source)
XLA Modules:
  0.0 30.1 jit_solution(4063848531041941134)
XLA Ops:
  0.0 0.8 %constant_dynamic-slice_fusion = (bf16[192,128]{1,0:T(8,128)(2,1)S(1)}, bf16[192,128]{1,0:T(8,128)(2,1)S(1)}) fusion(bf16[192,1024]{1,0:T(8,128)(2,1)} %param.6, s32[]{:T(128)S(6)} %select_n.15, bf16[192,1024]{1,0:T(8,128)(2,1)} %param.5), kind=kLoop, calls=%fused_computation.5 | loop fusion | bytes 196612 | tf_op jit(solution)/shard_map/dynamic_slice | solution.py:35
  0.8 0.7 %fusion.2 = bf16[192]{0:T(256)(128)(2,1)S(1)} fusion(s32[192]{0:T(256)} %param.7), kind=kLoop, calls=%fused_computation.4 | loop fusion | flops 1728 | bytes 1152 | tf_op jit(solution)/shard_map/convert_element_type | solution.py:37
  1.6 0.5 %collective-permute-start.1 = (bf16[208,256]{1,0:T(8,128)(2,1)S(1)}, bf16[208,256]{1,0:T(8,128)(2,1)S(1)}, u32[]{:S(2)}, u32[]{:S(2)}) collective-permute-start(bf16[208,256]{1,0:T(8,128)(2,1)S(1)} %fusion.1.refs_0_), channel_id=1, source_target_pairs={{1,0},{0,1},{3,2},{2,3},{5,4},{4,5},{7,6},{6,7},{9,8},{8,9},{11,10... | collective-permute-start | bytes 319496 | tf_op jit(solution)/shard_map/ppermute | solution.py:249
  2.1 2.6 %collective-permute-start = (bf16[208,256]{1,0:T(8,128)(2,1)S(1)}, bf16[208,256]{1,0:T(8,128)(2,1)S(1)}, u32[]{:S(2)}, u32[]{:S(2)}) collective-permute-start(bf16[208,256]{1,0:T(8,128)(2,1)S(1)} %fusion.1.refs_0_), channel_id=1, source_target_pairs={{2,0},{3,1},{0,2},{1,3},{6,4},{7,5},{4,6},{5,7},{10,8},{11,9},{8,1... | collective-permute-start | bytes 319496 | tf_op jit(solution)/shard_map/ppermute | solution.py:249
  4.7 0.0 collective-permute-done.1.refs_1_
  4.7 0.0 copy-start
  4.7 1.1 %copy-done = bf16[192,2048]{1,0:T(8,128)(2,1)S(1)} copy-done((bf16[192,2048]{1,0:T(8,128)(2,1)S(1)}, bf16[192,2048]{1,0:T(8,128)(2,1)}, u32[]{:S(2)}) %copy-start) | copy-done | bytes 786456
  5.8 2.1 %shard_map.46 = (f32[2,144,1536]{2,1,0:T(8,128)S(1)}, bf16[192,2048]{1,0:T(8,128)(2,1)S(1)}) custom-call(bf16[192,2048]{1,0:T(8,128)(2,1)S(1)} %copy-done, bf16[208,256]{1,0:T(8,128)(2,1)S(1)} %fusion.1.refs_0_, bf16[208,256]{1,0:T(8,128)(2,1)S(1)} %collective-permute-done.1.refs_1_), custom_call_target="tpu_custom_call" | custom-call | flops 603979776 | bytes 1572864 | tf_op jit(solution)/shard_map/pallas_call | solution.py:100
  7.9 0.4 %collective-permute-done.refs_2_ = bf16[208,256]{1,0:T(8,128)(2,1)S(1)} collective-permute-done((bf16[208,256]{1,0:T(8,128)(2,1)S(1)}, bf16[208,256]{1,0:T(8,128)(2,1)S(1)}, u32[]{:S(2)}, u32[]{:S(2)}) %collective-permute-start) | collective-permute-done | bytes 106528 | tf_op jit(solution)/shard_map/ppermute | solution.py:249
  8.2 0.0 collective-permute-start.2
  8.2 1.3 %collective-permute-done.2.refs_3_ = bf16[208,256]{1,0:T(8,128)(2,1)S(1)} collective-permute-done((bf16[208,256]{1,0:T(8,128)(2,1)S(1)}, bf16[208,256]{1,0:T(8,128)(2,1)S(1)}, u32[]{:S(2)}, u32[]{:S(2)}) %collective-permute-start.2) | collective-permute-done | bytes 106528 | tf_op jit(solution)/shard_map/ppermute | solution.py:249
  9.5 20.5 %shard_map.47 = bf16[192,2048]{1,0:T(8,128)(2,1)} custom-call(f32[2,144,1536]{2,1,0:T(8,128)S(1)} %get-tuple-element.16.sums_ref, bf16[192,2048]{1,0:T(8,128)(2,1)S(1)} %get-tuple-element.17.q_ref, bf16[208,256]{1,0:T(8,128)(2,1)S(1)} %fusion.1.refs_0_, bf16[208,256]{1,0:T(8,128)(2,1)S(1)} %collective-permute-done.1.refs_1_, ...), custom_call_target="tpu_custom_call" | custom-call | flops 603979776 | bytes 786432 | tf_op jit(solution)/shard_map/pallas_call | solution.py:225
  (2 shorter events, 0.0 us)
Async XLA Ops:
  1.6 3.1 %collective-permute-start.1 = (bf16[208,256]{1,0:T(8,128)(2,1)S(1)}, bf16[208,256]{1,0:T(8,128)(2,1)S(1)}, u32[]{:S(2)}, u32[]{:S(2)}) collective-permute-start(bf16[208,256]{1,0:T(8,128)(2,1)S(1)} %fusion.1.refs_0_), channel_id=1, source_target_pairs={{1,0},{0,1},{3,2},{2,3},{5,4},{4,5},{7,6},{6,7},{9,8},{8,9},{11,10... | collective-permute-start | bytes 319496 | tf_op jit(solution)/shard_map/ppermute | solution.py:249
  2.1 6.2 %collective-permute-start = (bf16[208,256]{1,0:T(8,128)(2,1)S(1)}, bf16[208,256]{1,0:T(8,128)(2,1)S(1)}, u32[]{:S(2)}, u32[]{:S(2)}) collective-permute-start(bf16[208,256]{1,0:T(8,128)(2,1)S(1)} %fusion.1.refs_0_), channel_id=1, source_target_pairs={{2,0},{3,1},{0,2},{1,3},{6,4},{7,5},{4,6},{5,7},{10,8},{11,9},{8,1... | collective-permute-start | bytes 319496 | tf_op jit(solution)/shard_map/ppermute | solution.py:249
  4.7 1.1 %copy-start = (bf16[192,2048]{1,0:T(8,128)(2,1)S(1)}, bf16[192,2048]{1,0:T(8,128)(2,1)}, u32[]{:S(2)}) copy-start(bf16[192,2048]{1,0:T(8,128)(2,1)} %queries_ref.1) | copy-start | bytes 2359300
  8.2 1.3 %collective-permute-start.2 = (bf16[208,256]{1,0:T(8,128)(2,1)S(1)}, bf16[208,256]{1,0:T(8,128)(2,1)S(1)}, u32[]{:S(2)}, u32[]{:S(2)}) collective-permute-start(bf16[208,256]{1,0:T(8,128)(2,1)S(1)} %collective-permute-done.refs_2_), channel_id=1, source_target_pairs={{1,0},{0,1},{3,2},{2,3},{5,4},{4,5},{7,6},{6,7},{9,8},{8,9},{11,10... | collective-permute-start | bytes 319496 | tf_op jit(solution)/shard_map/ppermute | solution.py:249

commit v3 on v2

--- a/solution.py
+++ b/solution.py
@@ -29,14 +29,39 @@
     return lax.dot_general(a, b, (((1,), (1,)), ((), ())), preferred_element_type=f32)
 
 
+def tail_kernel(tail_ref):
+    tail_ref[...] = jnp.zeros(tail_ref.shape, bf16)
+
+
+def join_kernel(keys_ref, values_ref, positions_ref, tail_ref, block_ref):
+    rows = keys_ref.shape[0]
+    block_ref[:rows, :HEAD_SIZE] = keys_ref[...]
+    block_ref[:rows, HEAD_SIZE:] = values_ref[...]
+    places = jnp.floor((positions_ref[...].astype(f32) + 0.5) * (1.0 / SPAN))
+    block_ref[rows:, :] = tail_ref[...]
+    block_ref[rows:, :rows] = jnp.broadcast_to(places, (TAIL, rows)).astype(bf16)
+
+
 def pack(keys, values, positions, heads):
     rows = keys.shape[0]
     group = lax.axis_index("head") * heads // QUERIES_PER_KV
+    tail = pl.pallas_call(
+        tail_kernel,
+        out_shape=jax.ShapeDtypeStruct((TAIL, 2 * HEAD_SIZE), bf16),
+        out_specs=in_vmem,
+        compiler_params=pltpu.CompilerParams(vmem_limit_bytes=VMEM_LIMIT),
+        cost_estimate=pl.CostEstimate(flops=2000000000, bytes_accessed=0, transcendentals=0),
+    )()
+    keys, values, tail = lax.optimization_barrier((keys, values, tail))
     ours = [lax.dynamic_slice_in_dim(a, group * HEAD_SIZE, HEAD_SIZE, 1) for a in (keys, values)]
-    *ours, positions = lax.optimization_barrier((*ours, positions))
-    places = (positions // SPAN).astype(bf16)[None]
-    places = jnp.pad(places, ((0, TAIL - 1), (0, 2 * HEAD_SIZE - rows)))
-    return jnp.concatenate([jnp.concatenate(ours, 1), places], 0)
+    return pl.pallas_call(
+        join_kernel,
+        out_shape=jax.ShapeDtypeStruct((rows + TAIL, 2 * HEAD_SIZE), bf16),
+        in_specs=[in_vmem] * 4,
+        out_specs=in_vmem,
+        compiler_params=pltpu.CompilerParams(vmem_limit_bytes=VMEM_LIMIT),
+        cost_estimate=pl.CostEstimate(flops=2000000000, bytes_accessed=4 * rows * HEAD_SIZE, transcendentals=0),
+    )(*ours, positions.reshape(1, rows), tail)
 
 
 def blocks_of(payloads, rows):
@@ -75,18 +100,12 @@
     return jnp.dot(values, weights.astype(bf16), preferred_element_type=f32)
 
 
-def first_kernel(queries_ref, *refs):
-    *payloads, sums_ref, q_ref, keys_ref, values_ref, spans_ref, sems = refs
+def first_kernel(q_ref, *refs):
+    *payloads, sums_ref, keys_ref, values_ref, spans_ref = refs
     rows = q_ref.shape[0]
     heads = q_ref.shape[1] // HEAD_SIZE
-    copies = []
-    for s in range(rows // SPAN):
-        here = pl.ds(s * SPAN, SPAN)
-        copies.append(pltpu.make_async_copy(queries_ref.at[here, :], q_ref.at[here, :], sems.at[s]))
-        copies[-1].start()
     unpack(payloads, rows, keys_ref, values_ref, spans_ref)
     for s in range(rows // SPAN):
-        copies[s].wait()
         span = spans_ref[:1, s * SPAN : s * SPAN + 1].astype(f32)
         sums_ref[s] = part(
             stacked(q_ref, s, heads), span, 0, keys_ref.shape[0], keys_ref, values_ref, spans_ref, s
@@ -99,17 +118,13 @@
     keys = sum(p.shape[0] for p in payloads) // (rows + TAIL) * rows
     return pl.pallas_call(
         first_kernel,
-        out_shape=(
-            jax.ShapeDtypeStruct((rows // SPAN, SUMS, heads * SPAN), f32),
-            jax.ShapeDtypeStruct(queries.shape, bf16),
-        ),
-        in_specs=[in_hbm] + [in_vmem] * len(payloads),
-        out_specs=(in_vmem, in_vmem),
+        out_shape=jax.ShapeDtypeStruct((rows // SPAN, SUMS, heads * SPAN), f32),
+        in_specs=[in_vmem] * (1 + len(payloads)),
+        out_specs=in_vmem,
         scratch_shapes=[
             pltpu.VMEM((keys, HEAD_SIZE), bf16),
             pltpu.VMEM((SUMS, keys), bf16),
             pltpu.VMEM((TAIL, keys), bf16),
-            pltpu.SemaphoreType.DMA((rows // SPAN,)),
         ],
         compiler_params=pltpu.CompilerParams(vmem_limit_bytes=VMEM_LIMIT),
         cost_estimate=pl.CostEstimate(
@@ -118,6 +133,42 @@
             transcendentals=rows * heads * keys,
         ),
     )(queries, *payloads)
+
+
+def middle_kernel(sums_ref, q_ref, own_ref, *refs):
+    *payloads, more_ref, keys_ref, values_ref, spans_ref = refs
+    rows = q_ref.shape[0]
+    heads = q_ref.shape[1] // HEAD_SIZE
+    unpack(payloads, rows, keys_ref, values_ref, spans_ref)
+    for s in range(rows // SPAN):
+        span = own_ref[rows : rows + 1, s * SPAN : s * SPAN + 1].astype(f32)
+        more_ref[s] = sums_ref[s] + part(
+            stacked(q_ref, s, heads), span, 0, keys_ref.shape[0], keys_ref, values_ref, spans_ref
+        )
+
+
+def middle_part(sums, queries, own, payloads):
+    rows = queries.shape[0]
+    heads = queries.shape[1] // HEAD_SIZE
+    keys = sum(p.shape[0] for p in payloads) // (rows + TAIL) * rows
+    return pl.pallas_call(
+        middle_kernel,
+        out_shape=jax.ShapeDtypeStruct(sums.shape, f32),
+        in_specs=[in_vmem] * (3 + len(payloads)),
+        out_specs=in_vmem,
+        scratch_shapes=[
+            pltpu.VMEM((keys, HEAD_SIZE), bf16),
+            pltpu.VMEM((SUMS, keys), bf16),
+            pltpu.VMEM((TAIL, keys), bf16),
+        ],
+        input_output_aliases={0: 0},
+        compiler_params=pltpu.CompilerParams(vmem_limit_bytes=VMEM_LIMIT),
+        cost_estimate=pl.CostEstimate(
+            flops=4 * rows * heads * keys * HEAD_SIZE,
+            bytes_accessed=2 * rows * heads * HEAD_SIZE,
+            transcendentals=rows * heads * keys,
+        ),
+    )(sums, queries, own, *payloads)
 
 
 def last_kernel(held, group, sums_ref, q_ref, *refs):
@@ -250,22 +301,22 @@
 
 
 def body(queries, rotated_key_rows, value_state_rows, positions):
-    heads_here = queries.shape[1] // HEAD_SIZE
-    own = pack(rotated_key_rows, value_state_rows, positions, heads_here)
+    own = pack(rotated_key_rows, value_state_rows, positions, queries.shape[1] // HEAD_SIZE)
     size = lax.axis_size("ctx")
     if size == 4:
-        core = swapped(own, 1)
         chip = swapped(own, 2)
-        sums, q = first_part(queries, [own, core])
-        chip, sums = lax.optimization_barrier((chip, sums))
+        sums = first_part(queries, [own])
+        again, sums = lax.optimization_barrier((own, sums))
+        core = swapped(again, 1)
         both = swapped(chip, 1)
-        return last_part(sums, q, [own, core, chip, both], 2, 2)
+        sums = middle_part(sums, queries, own, [core, chip])
+        return last_part(sums, queries, [own, core, chip, both], 3, 1)
     everyone = lax.all_gather(own, "ctx", axis=0)
     others = (lax.axis_index("ctx") + jnp.arange(1, size)) % size
     others = jnp.take(everyone, others, axis=0)
     rest = others[1:].reshape(-1, 2 * HEAD_SIZE)
-    sums, q = first_part(queries, [own, others[0]])
-    return last_part(sums, q, [own, others[0], rest], 2, 2)
+    sums = first_part(queries, [own, others[0]])
+    return last_part(sums, queries, [own, others[0], rest], 2, 2)
 
 
 def solution(mesh):

time: 30.3 us -> 28.7 us (0.947)
  local copies, waits for them, and re-layouts: 1.97 us -> 0.85 us
  other arithmetic: 0.71 us -> 0 us
    unnamed x2 -> x4, local copies, waits for them, and re-layouts: 1.13 us -> 0.01 us
    convert_element_type x1 -> x0, other arithmetic: 0.69 us -> none  [pack(): places = (positions // SPAN).astype(bf16)[None]]
    pallas_call x1, Pallas kernels: 20.5 us -> 20.2 us  [last_part(): pl.pallas_call(functools.partial(last_kernel, held, group_blocks * rows),...]
    pallas_call x1 -> x4, Pallas kernels: 2.06 us -> 2.4 us  [the longest x1 1.42 us: middle_part(): pl.pallas_call(middle_kernel, out_shape=jax.ShapeDtypeStruct(sums.shape,...]
  transfers between devices with their start and end apart: 3 -> 3, of which waited for: 2 -> 1; matrix products, arithmetic and copies ran while one was open for 0% -> 0% of each run, Pallas kernels for 7% -> 8%
where the time goes in v3:
time: 28.7 us; the launch traced here: 28.5 us
  Pallas kernels  22.6 us (79%)
  starting transfers between devices  3.11 us (11%)
  waiting for transfers between devices  1.94 us (7%)
  local copies, waits for them, and re-layouts  0.85 us (3%)
    pallas_call x1, Pallas kernels, last_part(): pl.pallas_call(functools.partial(last_kernel, held, group_blocks * rows),...  20.2 us
    ppermute x3, starting transfers between devices, swapped(): return lax.ppermute(block, 'ctx', [(i ^ bit, i) for i in devices])  3.11 us
    ppermute x3, waiting for transfers between devices, swapped(): return lax.ppermute(block, 'ctx', [(i ^ bit, i) for i in devices])  1.94 us
    pallas_call x1, Pallas kernels, middle_part(): pl.pallas_call(middle_kernel, out_shape=jax.ShapeDtypeStruct(sums.shape,...  1.42 us
    pallas_call x1, Pallas kernels, first_part(): pl.pallas_call(first_kernel, out_shape=jax.ShapeDtypeStruct((rows // SPAN...  0.95 us
    dynamic_slice x1, local copies, waits for them, and re-layouts, pack(): lax.dynamic_slice_in_dim(a, group * HEAD_SIZE, HEAD_SIZE, 1)  0.84 us
  transfers between devices with their start and end apart: 3, of which 1 were waited for; matrix products, arithmetic and copies ran while one was open for 0% of the time, Pallas kernels for 8%

profile of v3, /device:TPU:0, one launch (start us, length us, event | category | flops | bytes accessed | tf_op | source)
XLA Modules:
  0.0 28.5 jit_solution(17369975045557658868)
XLA Ops:
  0.0 0.0 copy-start.1
  0.0 0.8 %constant_dynamic-slice_fusion = (bf16[192,128]{1,0:T(8,128)(2,1)S(1)}, bf16[192,128]{1,0:T(8,128)(2,1)S(1)}) fusion(bf16[192,1024]{1,0:T(8,128)(2,1)} %param.6, s32[]{:T(128)S(6)} %select_n.10, bf16[192,1024]{1,0:T(8,128)(2,1)} %param.5), kind=kLoop, calls=%fused_computation | loop fusion | bytes 196612 | tf_op jit(solution)/shard_map/dynamic_slice | solution.py:56
  0.8 0.0 copy-done.1
  0.9 0.0 copy-start
  0.9 3.0 %collective-permute-start.1 = (bf16[208,256]{1,0:T(8,128)(2,1)S(1)}, bf16[208,256]{1,0:T(8,128)(2,1)S(1)}, u32[]{:S(2)}, u32[]{:S(2)}) collective-permute-start(bf16[208,256]{1,0:T(8,128)(2,1)S(1)} %shard_map.47.refs_0_.own_ref), channel_id=1, source_target_pairs={{2,0},{3,1},{0,2},{1,3},{6,4},{7,5},{4,6},{5,7},{10,8},{11,9},{8,1... | collective-permute-start | bytes 319496 | tf_op jit(solution)/shard_map/ppermute | solution.py:300
  3.9 0.0 copy-done
  3.9 0.9 %shard_map.48.sums_ref = f32[2,144,1536]{2,1,0:T(8,128)S(1)} custom-call(bf16[192,2048]{1,0:T(8,128)(2,1)S(1)} %copy-done, bf16[208,256]{1,0:T(8,128)(2,1)S(1)} %shard_map.47.refs_0_.own_ref), custom_call_target="tpu_custom_call" | custom-call | flops 301989888 | bytes 1572864 | tf_op jit(solution)/shard_map/pallas_call | solution.py:119
  4.9 0.1 collective-permute-start
  5.0 1.9 %collective-permute-done.1.refs_1_.refs_2_ = bf16[208,256]{1,0:T(8,128)(2,1)S(1)} collective-permute-done((bf16[208,256]{1,0:T(8,128)(2,1)S(1)}, bf16[208,256]{1,0:T(8,128)(2,1)S(1)}, u32[]{:S(2)}, u32[]{:S(2)}) %collective-permute-start.1) | collective-permute-done | bytes 106528 | tf_op jit(solution)/shard_map/ppermute | solution.py:300
  6.9 0.0 collective-permute-start.2
  6.9 0.0 collective-permute-done.refs_0_.refs_1_
  6.9 1.4 %shard_map.49.sums_ref = f32[2,144,1536]{2,1,0:T(8,128)S(1)} custom-call(f32[2,144,1536]{2,1,0:T(8,128)S(1)} %shard_map.48.sums_ref, bf16[192,2048]{1,0:T(8,128)(2,1)S(1)} %copy-done, bf16[208,256]{1,0:T(8,128)(2,1)S(1)} %shard_map.47.refs_0_.own_ref, bf16[208,256]{1,0:T(8,128)(2,1)S(1)} %collective-permute-done.refs_0_.refs_1_, ...), custom_call_target="tpu_custom_call", output_to_operand_aliasing={{}: (0, {})} | custom-call | flops 603979776 | bytes 786432 | tf_op jit(solution)/shard_map/pallas_call | solution.py:154
  8.3 0.0 collective-permute-done.2.refs_3_
  8.3 20.2 %shard_map.50 = bf16[192,2048]{1,0:T(8,128)(2,1)} custom-call(f32[2,144,1536]{2,1,0:T(8,128)S(1)} %shard_map.49.sums_ref, bf16[192,2048]{1,0:T(8,128)(2,1)S(1)} %copy-done, bf16[208,256]{1,0:T(8,128)(2,1)S(1)} %shard_map.47.refs_0_.own_ref, bf16[208,256]{1,0:T(8,128)(2,1)S(1)} %collective-permute-done.refs_0_.refs_1_, ...), custom_call_target="tpu_custom_call" | custom-call | flops 301989888 | bytes 786432 | tf_op jit(solution)/shard_map/pallas_call | solution.py:276
  (2 shorter events, 0.0 us)
Async XLA Ops:
  0.0 0.8 %copy-start.1 = (s32[192]{0:T(256)S(1)}, s32[192]{0:T(256)}, u32[]{:S(2)}) copy-start(s32[192]{0:T(256)} %param.7) | copy-start | bytes 2308
  0.9 3.1 %copy-start = (bf16[192,2048]{1,0:T(8,128)(2,1)S(1)}, bf16[192,2048]{1,0:T(8,128)(2,1)}, u32[]{:S(2)}) copy-start(bf16[192,2048]{1,0:T(8,128)(2,1)} %q_ref.5) | copy-start | bytes 2359300
  0.9 6.0 %collective-permute-start.1 = (bf16[208,256]{1,0:T(8,128)(2,1)S(1)}, bf16[208,256]{1,0:T(8,128)(2,1)S(1)}, u32[]{:S(2)}, u32[]{:S(2)}) collective-permute-start(bf16[208,256]{1,0:T(8,128)(2,1)S(1)} %shard_map.47.refs_0_.own_ref), channel_id=1, source_target_pairs={{2,0},{3,1},{0,2},{1,3},{6,4},{7,5},{4,6},{5,7},{10,8},{11,9},{8,1... | collective-permute-start | bytes 319496 | tf_op jit(solution)/shard_map/ppermute | solution.py:300
  4.9 2.0 %collective-permute-start = (bf16[208,256]{1,0:T(8,128)(2,1)S(1)}, bf16[208,256]{1,0:T(8,128)(2,1)S(1)}, u32[]{:S(2)}, u32[]{:S(2)}) collective-permute-start(bf16[208,256]{1,0:T(8,128)(2,1)S(1)} %shard_map.47.refs_0_.own_ref), channel_id=1, source_target_pairs={{1,0},{0,1},{3,2},{2,3},{5,4},{4,5},{7,6},{6,7},{9,8},{8,9},{11,10... | collective-permute-start | bytes 319496 | tf_op jit(solution)/shard_map/ppermute | solution.py:300
  6.9 1.4 %collective-permute-start.2 = (bf16[208,256]{1,0:T(8,128)(2,1)S(1)}, bf16[208,256]{1,0:T(8,128)(2,1)S(1)}, u32[]{:S(2)}, u32[]{:S(2)}) collective-permute-start(bf16[208,256]{1,0:T(8,128)(2,1)S(1)} %collective-permute-done.1.refs_1_.refs_2_), channel_id=1, source_target_pairs={{1,0},{0,1},{3,2},{2,3},{5,4},{4,5},{7,6},{6,7},{9,8},{8,9},{11,10... | collective-permute-start | bytes 319496 | tf_op jit(solution)/shard_map/ppermute | solution.py:300

commit v4 on v3

--- a/solution.py
+++ b/solution.py
@@ -18,6 +18,7 @@
 LEAST_TOTAL = 1e-25
 LARGEST_TOTAL = 1e25
 VMEM_LIMIT = 40 << 20
+PIECES = 2
 
 f32 = jnp.float32
 bf16 = jnp.bfloat16
@@ -179,10 +180,11 @@
     own = payloads[0]
     unpack(payloads[held:], rows, keys_ref, values_ref, spans_ref)
     groups = keys_ref.shape[0] // group
-
-    def copy(s):
-        here = pl.ds(s * SPAN, SPAN)
-        return pltpu.make_async_copy(ready_ref.at[here, :], out_ref.at[here, :], sems.at[s])
+    wide = q_ref.shape[1] // PIECES
+
+    def copy(s, piece):
+        at = (pl.ds(s * SPAN, SPAN), pl.ds(piece * wide, wide))
+        return pltpu.make_async_copy(ready_ref.at[at], out_ref.at[at], sems.at[s, piece])
 
     fine = None
     for s in range(spans):
@@ -202,14 +204,21 @@
         total = summed[HEAD_SIZE : HEAD_SIZE + 1]
         inside = jnp.where((total >= LEAST_TOTAL) & (total <= LARGEST_TOTAL), 1.0, 0.0)
         fine = inside if fine is None else jnp.minimum(fine, inside)
-        attended = (summed[:HEAD_SIZE] * (1.0 / total)).T.astype(bf16)
-        for h in range(heads):
-            ready_ref[here, h * HEAD_SIZE : (h + 1) * HEAD_SIZE] = attended[h * SPAN : (h + 1) * SPAN]
-        copy(s).start()
+        inverse = 1.0 / total
+        some = heads // PIECES
+        for piece in range(PIECES):
+            across = slice(piece * some * SPAN, (piece + 1) * some * SPAN)
+            attended = (summed[:HEAD_SIZE, across] * inverse[:, across]).T.astype(bf16)
+            for h in range(some):
+                at = (piece * some + h) * HEAD_SIZE
+                ready_ref[here, at : at + HEAD_SIZE] = attended[h * SPAN : (h + 1) * SPAN]
+            copy(s, piece).start()
+    unsafe = jnp.min(fine) < 0.5
     for s in range(spans):
-        copy(s).wait()
-
-    @pl.when(jnp.min(fine) < 0.5)
+        for piece in range(PIECES):
+            copy(s, piece).wait()
+
+    @pl.when(unsafe)
     def _():
         @pl.loop(0, heads)
         def _(h):
@@ -218,9 +227,11 @@
                 careful(payloads, q_ref, ready_ref, s, at)
 
         for s in range(spans):
-            copy(s).start()
+            for piece in range(PIECES):
+                copy(s, piece).start()
         for s in range(spans):
-            copy(s).wait()
+            for piece in range(PIECES):
+                copy(s, piece).wait()
 
 
 def careful(payloads, q_ref, ready_ref, s, at):
@@ -284,7 +295,7 @@
             pltpu.VMEM((TAIL, keys), bf16),
             pltpu.VMEM((SUMS, heads * SPAN) if keys > group_blocks * rows else (8, HEAD_SIZE), f32),
             pltpu.VMEM(queries.shape, bf16),
-            pltpu.SemaphoreType.DMA((rows // SPAN,)),
+            pltpu.SemaphoreType.DMA((rows // SPAN, PIECES)),
         ],
         compiler_params=pltpu.CompilerParams(vmem_limit_bytes=VMEM_LIMIT),
         cost_estimate=pl.CostEstimate(

time: 28.7 us -> 28.5 us (level)
  no operation moved by 1% of the time
where the time goes in v4:
time: 28.5 us; the launch traced here: 28.3 us
  Pallas kernels  22.4 us (79%)
  starting transfers between devices  3.11 us (11%)
  waiting for transfers between devices  1.94 us (7%)
  local copies, waits for them, and re-layouts  0.85 us (3%)
    pallas_call x1, Pallas kernels, last_part(): pl.pallas_call(functools.partial(last_kernel, held, group_blocks * rows),...  20 us
    ppermute x3, starting transfers between devices, swapped(): return lax.ppermute(block, 'ctx', [(i ^ bit, i) for i in devices])  3.11 us
    ppermute x3, waiting for transfers between devices, swapped(): return lax.ppermute(block, 'ctx', [(i ^ bit, i) for i in devices])  1.94 us
    pallas_call x1, Pallas kernels, middle_part(): pl.pallas_call(middle_kernel, out_shape=jax.ShapeDtypeStruct(sums.shape,...  1.42 us
    pallas_call x1, Pallas kernels, first_part(): pl.pallas_call(first_kernel, out_shape=jax.ShapeDtypeStruct((rows // SPAN...  0.95 us
    dynamic_slice x1, local copies, waits for them, and re-layouts, pack(): lax.dynamic_slice_in_dim(a, group * HEAD_SIZE, HEAD_SIZE, 1)  0.84 us
  transfers between devices with their start and end apart: 3, of which 1 were waited for; matrix products, arithmetic and copies ran while one was open for 0% of the time, Pallas kernels for 8%

profile of v4, /device:TPU:0, one launch (start us, length us, event | category | flops | bytes accessed | tf_op | source)
XLA Modules:
  0.0 28.3 jit_solution(13164297643889028051)
XLA Ops:
  0.0 0.0 copy-start.1
  0.0 0.8 %constant_dynamic-slice_fusion = (bf16[192,128]{1,0:T(8,128)(2,1)S(1)}, bf16[192,128]{1,0:T(8,128)(2,1)S(1)}) fusion(bf16[192,1024]{1,0:T(8,128)(2,1)} %param.6, s32[]{:T(128)S(6)} %select_n.10, bf16[192,1024]{1,0:T(8,128)(2,1)} %param.5), kind=kLoop, calls=%fused_computation | loop fusion | bytes 196612 | tf_op jit(solution)/shard_map/dynamic_slice | solution.py:57
  0.8 0.0 copy-done.1
  0.9 0.0 copy-start
  0.9 3.0 %collective-permute-start.1 = (bf16[208,256]{1,0:T(8,128)(2,1)S(1)}, bf16[208,256]{1,0:T(8,128)(2,1)S(1)}, u32[]{:S(2)}, u32[]{:S(2)}) collective-permute-start(bf16[208,256]{1,0:T(8,128)(2,1)S(1)} %shard_map.47.refs_0_.own_ref), channel_id=1, source_target_pairs={{2,0},{3,1},{0,2},{1,3},{6,4},{7,5},{4,6},{5,7},{10,8},{11,9},{8,1... | collective-permute-start | bytes 319496 | tf_op jit(solution)/shard_map/ppermute | solution.py:311
  3.9 0.0 copy-done
  3.9 0.9 %shard_map.48.sums_ref = f32[2,144,1536]{2,1,0:T(8,128)S(1)} custom-call(bf16[192,2048]{1,0:T(8,128)(2,1)S(1)} %copy-done, bf16[208,256]{1,0:T(8,128)(2,1)S(1)} %shard_map.47.refs_0_.own_ref), custom_call_target="tpu_custom_call" | custom-call | flops 301989888 | bytes 1572864 | tf_op jit(solution)/shard_map/pallas_call | solution.py:120
  4.9 0.1 collective-permute-start
  5.0 1.9 %collective-permute-done.1.refs_1_.refs_2_ = bf16[208,256]{1,0:T(8,128)(2,1)S(1)} collective-permute-done((bf16[208,256]{1,0:T(8,128)(2,1)S(1)}, bf16[208,256]{1,0:T(8,128)(2,1)S(1)}, u32[]{:S(2)}, u32[]{:S(2)}) %collective-permute-start.1) | collective-permute-done | bytes 106528 | tf_op jit(solution)/shard_map/ppermute | solution.py:311
  6.9 0.0 collective-permute-start.2
  6.9 0.0 collective-permute-done.refs_0_.refs_1_
  6.9 1.4 %shard_map.49.sums_ref = f32[2,144,1536]{2,1,0:T(8,128)S(1)} custom-call(f32[2,144,1536]{2,1,0:T(8,128)S(1)} %shard_map.48.sums_ref, bf16[192,2048]{1,0:T(8,128)(2,1)S(1)} %copy-done, bf16[208,256]{1,0:T(8,128)(2,1)S(1)} %shard_map.47.refs_0_.own_ref, bf16[208,256]{1,0:T(8,128)(2,1)S(1)} %collective-permute-done.refs_0_.refs_1_, ...), custom_call_target="tpu_custom_call", output_to_operand_aliasing={{}: (0, {})} | custom-call | flops 603979776 | bytes 786432 | tf_op jit(solution)/shard_map/pallas_call | solution.py:155
  8.3 0.0 collective-permute-done.2.refs_3_
  8.3 20.0 %shard_map.50 = bf16[192,2048]{1,0:T(8,128)(2,1)} custom-call(f32[2,144,1536]{2,1,0:T(8,128)S(1)} %shard_map.49.sums_ref, bf16[192,2048]{1,0:T(8,128)(2,1)S(1)} %copy-done, bf16[208,256]{1,0:T(8,128)(2,1)S(1)} %shard_map.47.refs_0_.own_ref, bf16[208,256]{1,0:T(8,128)(2,1)S(1)} %collective-permute-done.refs_0_.refs_1_, ...), custom_call_target="tpu_custom_call" | custom-call | flops 301989888 | bytes 786432 | tf_op jit(solution)/shard_map/pallas_call | solution.py:287
  (2 shorter events, 0.0 us)
Async XLA Ops:
  0.0 0.8 %copy-start.1 = (s32[192]{0:T(256)S(1)}, s32[192]{0:T(256)}, u32[]{:S(2)}) copy-start(s32[192]{0:T(256)} %param.7) | copy-start | bytes 2308
  0.9 3.1 %copy-start = (bf16[192,2048]{1,0:T(8,128)(2,1)S(1)}, bf16[192,2048]{1,0:T(8,128)(2,1)}, u32[]{:S(2)}) copy-start(bf16[192,2048]{1,0:T(8,128)(2,1)} %q_ref.5) | copy-start | bytes 2359300
  0.9 6.0 %collective-permute-start.1 = (bf16[208,256]{1,0:T(8,128)(2,1)S(1)}, bf16[208,256]{1,0:T(8,128)(2,1)S(1)}, u32[]{:S(2)}, u32[]{:S(2)}) collective-permute-start(bf16[208,256]{1,0:T(8,128)(2,1)S(1)} %shard_map.47.refs_0_.own_ref), channel_id=1, source_target_pairs={{2,0},{3,1},{0,2},{1,3},{6,4},{7,5},{4,6},{5,7},{10,8},{11,9},{8,1... | collective-permute-start | bytes 319496 | tf_op jit(solution)/shard_map/ppermute | solution.py:311
  4.9 2.0 %collective-permute-start = (bf16[208,256]{1,0:T(8,128)(2,1)S(1)}, bf16[208,256]{1,0:T(8,128)(2,1)S(1)}, u32[]{:S(2)}, u32[]{:S(2)}) collective-permute-start(bf16[208,256]{1,0:T(8,128)(2,1)S(1)} %shard_map.47.refs_0_.own_ref), channel_id=1, source_target_pairs={{1,0},{0,1},{3,2},{2,3},{5,4},{4,5},{7,6},{6,7},{9,8},{8,9},{11,10... | collective-permute-start | bytes 319496 | tf_op jit(solution)/shard_map/ppermute | solution.py:311
  6.9 1.4 %collective-permute-start.2 = (bf16[208,256]{1,0:T(8,128)(2,1)S(1)}, bf16[208,256]{1,0:T(8,128)(2,1)S(1)}, u32[]{:S(2)}, u32[]{:S(2)}) collective-permute-start(bf16[208,256]{1,0:T(8,128)(2,1)S(1)} %collective-permute-done.1.refs_1_.refs_2_), channel_id=1, source_target_pairs={{1,0},{0,1},{3,2},{2,3},{5,4},{4,5},{7,6},{6,7},{9,8},{8,9},{11,10... | collective-permute-start | bytes 319496 | tf_op jit(solution)/shard_map/ppermute | solution.py:311

commit v5 on v4

--- a/solution.py
+++ b/solution.py
@@ -88,17 +88,26 @@
 
 
 def part(q, span, first, count, keys_ref, values_ref, spans_ref, own=None):
+    weights = weigh(q, first, count, keys_ref, own)
+    return gather(weights, span, first, count, values_ref, spans_ref)
+
+
+def gather(weights, span, first, count, values_ref, spans_ref):
     some = pl.ds(first, count)
     allowed = (spans_ref[:1, some].astype(f32) <= span).astype(f32).astype(bf16)
     values = values_ref[:, some] * allowed
-    weights = jnp.exp2(nt(keys_ref[some, :], q) * SCALE_TWO)
+    return jnp.dot(values, weights, preferred_element_type=f32)
+
+
+def weigh(q, first, count, keys_ref, own=None):
+    weights = jnp.exp2(nt(keys_ref[pl.ds(first, count), :], q) * SCALE_TWO)
     if own is not None:
         key = lax.broadcasted_iota(jnp.int32, (SPAN, q.shape[0]), 0)
         query = lax.broadcasted_iota(jnp.int32, (SPAN, q.shape[0]), 1) % SPAN
         low, high = own * SPAN, (own + 1) * SPAN
         pieces = [weights[:low], jnp.where(key <= query, weights[low:high], 0.0), weights[high:]]
         weights = jnp.concatenate([p for p in pieces if p.shape[0]], 0)
-    return jnp.dot(values, weights.astype(bf16), preferred_element_type=f32)
+    return weights.astype(bf16)
 
 
 def first_kernel(q_ref, *refs):
@@ -106,11 +115,11 @@
     rows = q_ref.shape[0]
     heads = q_ref.shape[1] // HEAD_SIZE
     unpack(payloads, rows, keys_ref, values_ref, spans_ref)
-    for s in range(rows // SPAN):
+    keys = keys_ref.shape[0]
+    weights = [weigh(stacked(q_ref, s, heads), 0, keys, keys_ref, s) for s in range(rows // SPAN)]
+    for s, some in enumerate(weights):
         span = spans_ref[:1, s * SPAN : s * SPAN + 1].astype(f32)
-        sums_ref[s] = part(
-            stacked(q_ref, s, heads), span, 0, keys_ref.shape[0], keys_ref, values_ref, spans_ref, s
-        )
+        sums_ref[s] = gather(some, span, 0, keys, values_ref, spans_ref)
 
 
 def first_part(queries, payloads):
@@ -141,11 +150,11 @@
     rows = q_ref.shape[0]
     heads = q_ref.shape[1] // HEAD_SIZE
     unpack(payloads, rows, keys_ref, values_ref, spans_ref)
-    for s in range(rows // SPAN):
+    keys = keys_ref.shape[0]
+    weights = [weigh(stacked(q_ref, s, heads), 0, keys, keys_ref) for s in range(rows // SPAN)]
+    for s, some in enumerate(weights):
         span = own_ref[rows : rows + 1, s * SPAN : s * SPAN + 1].astype(f32)
-        more_ref[s] = sums_ref[s] + part(
-            stacked(q_ref, s, heads), span, 0, keys_ref.shape[0], keys_ref, values_ref, spans_ref
-        )
+        more_ref[s] = sums_ref[s] + gather(some, span, 0, keys, values_ref, spans_ref)
 
 
 def middle_part(sums, queries, own, payloads):
@@ -186,21 +195,25 @@
         at = (pl.ds(s * SPAN, SPAN), pl.ds(piece * wide, wide))
         return pltpu.make_async_copy(ready_ref.at[at], out_ref.at[at], sems.at[s, piece])
 
+    weights = [weigh(stacked(q_ref, s, heads), 0, group, keys_ref) for s in range(spans if groups == 1 else 0)]
+    sums = []
+    for s in range(spans):
+        span = own[rows : rows + 1, s * SPAN : s * SPAN + 1].astype(f32)
+        if groups == 1:
+            sums.append(sums_ref[s] + gather(weights[s], span, 0, group, values_ref, spans_ref))
+            continue
+        q = stacked(q_ref, s, heads)
+        acc_ref[...] = sums_ref[s]
+
+        @pl.loop(0, groups)
+        def _(g):
+            first = pl.multiple_of(g * group, group)
+            acc_ref[...] += part(q, span, first, group, keys_ref, values_ref, spans_ref)
+
+        sums.append(acc_ref[...])
     fine = None
-    for s in range(spans):
+    for s, summed in enumerate(sums):
         here = slice(s * SPAN, (s + 1) * SPAN)
-        span = own[rows : rows + 1, s * SPAN : s * SPAN + 1].astype(f32)
-        q = stacked(q_ref, s, heads)
-        summed = sums_ref[s] + part(q, span, 0, group, keys_ref, values_ref, spans_ref)
-        if groups > 1:
-            acc_ref[...] = summed
-
-            @pl.loop(1, groups)
-            def _(g):
-                first = pl.multiple_of(g * group, group)
-                acc_ref[...] += part(q, span, first, group, keys_ref, values_ref, spans_ref)
-
-            summed = acc_ref[...]
         total = summed[HEAD_SIZE : HEAD_SIZE + 1]
         inside = jnp.where((total >= LEAST_TOTAL) & (total <= LARGEST_TOTAL), 1.0, 0.0)
         fine = inside if fine is None else jnp.minimum(fine, inside)
@@ -208,7 +221,7 @@
         some = heads // PIECES
         for piece in range(PIECES):
             across = slice(piece * some * SPAN, (piece + 1) * some * SPAN)
-            attended = (summed[:HEAD_SIZE, across] * inverse[:, across]).T.astype(bf16)
+            attended = (summed[:HEAD_SIZE, across] * inverse[:, across]).astype(bf16).T
             for h in range(some):
                 at = (piece * some + h) * HEAD_SIZE
                 ready_ref[here, at : at + HEAD_SIZE] = attended[h * SPAN : (h + 1) * SPAN]

time: 28.5 us -> 28.3 us (level)
  Pallas kernels: 22.4 us -> 22 us
where the time goes in v5:
time: 28.3 us; the launch traced here: 28.1 us
  Pallas kernels  22 us (78%)
  starting transfers between devices  3.11 us (11%)
  waiting for transfers between devices  2.07 us (7%)
  local copies, waits for them, and re-layouts  0.85 us (3%)
    pallas_call x1, Pallas kernels, last_part(): pl.pallas_call(functools.partial(last_kernel, held, group_blocks * rows),...  19.8 us
    ppermute x3, starting transfers between devices, swapped(): return lax.ppermute(block, 'ctx', [(i ^ bit, i) for i in devices])  3.11 us
    ppermute x3, waiting for transfers between devices, swapped(): return lax.ppermute(block, 'ctx', [(i ^ bit, i) for i in devices])  2.07 us
    pallas_call x1, Pallas kernels, middle_part(): pl.pallas_call(middle_kernel, out_shape=jax.ShapeDtypeStruct(sums.shape,...  1.42 us
    dynamic_slice x1, local copies, waits for them, and re-layouts, pack(): lax.dynamic_slice_in_dim(a, group * HEAD_SIZE, HEAD_SIZE, 1)  0.84 us
    pallas_call x1, Pallas kernels, first_part(): pl.pallas_call(first_kernel, out_shape=jax.ShapeDtypeStruct((rows // SPAN...  0.81 us
  transfers between devices with their start and end apart: 3, of which 1 were waited for; matrix products, arithmetic and copies ran while one was open for 0% of the time, Pallas kernels for 8%

profile of v5, /device:TPU:0, one launch (start us, length us, event | category | flops | bytes accessed | tf_op | source)
XLA Modules:
  0.0 28.1 jit_solution(11843570167504239406)
XLA Ops:
  0.0 0.0 copy-start.1
  0.0 0.8 %constant_dynamic-slice_fusion = (bf16[192,128]{1,0:T(8,128)(2,1)S(1)}, bf16[192,128]{1,0:T(8,128)(2,1)S(1)}) fusion(bf16[192,1024]{1,0:T(8,128)(2,1)} %param.6, s32[]{:T(128)S(6)} %select_n.10, bf16[192,1024]{1,0:T(8,128)(2,1)} %param.5), kind=kLoop, calls=%fused_computation | loop fusion | bytes 196612 | tf_op jit(solution)/shard_map/dynamic_slice | solution.py:57
  0.8 0.0 copy-done.1
  0.9 0.0 copy-start
  0.9 3.0 %collective-permute-start.1 = (bf16[208,256]{1,0:T(8,128)(2,1)S(1)}, bf16[208,256]{1,0:T(8,128)(2,1)S(1)}, u32[]{:S(2)}, u32[]{:S(2)}) collective-permute-start(bf16[208,256]{1,0:T(8,128)(2,1)S(1)} %shard_map.47.refs_0_.own_ref), channel_id=1, source_target_pairs={{2,0},{3,1},{0,2},{1,3},{6,4},{7,5},{4,6},{5,7},{10,8},{11,9},{8,1... | collective-permute-start | bytes 319496 | tf_op jit(solution)/shard_map/ppermute | solution.py:324
  3.9 0.0 copy-done
  3.9 0.8 %shard_map.48.sums_ref = f32[2,144,1536]{2,1,0:T(8,128)S(1)} custom-call(bf16[192,2048]{1,0:T(8,128)(2,1)S(1)} %copy-done, bf16[208,256]{1,0:T(8,128)(2,1)S(1)} %shard_map.47.refs_0_.own_ref), custom_call_target="tpu_custom_call" | custom-call | flops 301989888 | bytes 1572864 | tf_op jit(solution)/shard_map/pallas_call | solution.py:129
  4.8 0.1 collective-permute-start
  4.8 2.1 %collective-permute-done.1.refs_1_.refs_2_ = bf16[208,256]{1,0:T(8,128)(2,1)S(1)} collective-permute-done((bf16[208,256]{1,0:T(8,128)(2,1)S(1)}, bf16[208,256]{1,0:T(8,128)(2,1)S(1)}, u32[]{:S(2)}, u32[]{:S(2)}) %collective-permute-start.1) | collective-permute-done | bytes 106528 | tf_op jit(solution)/shard_map/ppermute | solution.py:324
  6.9 0.0 collective-permute-start.2
  6.9 0.0 collective-permute-done.refs_0_.refs_1_
  6.9 1.4 %shard_map.49.sums_ref = f32[2,144,1536]{2,1,0:T(8,128)S(1)} custom-call(f32[2,144,1536]{2,1,0:T(8,128)S(1)} %shard_map.48.sums_ref, bf16[192,2048]{1,0:T(8,128)(2,1)S(1)} %copy-done, bf16[208,256]{1,0:T(8,128)(2,1)S(1)} %shard_map.47.refs_0_.own_ref, bf16[208,256]{1,0:T(8,128)(2,1)S(1)} %collective-permute-done.refs_0_.refs_1_, ...), custom_call_target="tpu_custom_call", output_to_operand_aliasing={{}: (0, {})} | custom-call | flops 603979776 | bytes 786432 | tf_op jit(solution)/shard_map/pallas_call | solution.py:164
  8.3 0.0 collective-permute-done.2.refs_3_
  8.3 19.8 %shard_map.50 = bf16[192,2048]{1,0:T(8,128)(2,1)} custom-call(f32[2,144,1536]{2,1,0:T(8,128)S(1)} %shard_map.49.sums_ref, bf16[192,2048]{1,0:T(8,128)(2,1)S(1)} %copy-done, bf16[208,256]{1,0:T(8,128)(2,1)S(1)} %shard_map.47.refs_0_.own_ref, bf16[208,256]{1,0:T(8,128)(2,1)S(1)} %collective-permute-done.refs_0_.refs_1_, ...), custom_call_target="tpu_custom_call" | custom-call | flops 301989888 | bytes 786432 | tf_op jit(solution)/shard_map/pallas_call | solution.py:300
  (2 shorter events, 0.0 us)
Async XLA Ops:
  0.0 0.8 %copy-start.1 = (s32[192]{0:T(256)S(1)}, s32[192]{0:T(256)}, u32[]{:S(2)}) copy-start(s32[192]{0:T(256)} %param.7) | copy-start | bytes 2308
  0.9 3.1 %copy-start = (bf16[192,2048]{1,0:T(8,128)(2,1)S(1)}, bf16[192,2048]{1,0:T(8,128)(2,1)}, u32[]{:S(2)}) copy-start(bf16[192,2048]{1,0:T(8,128)(2,1)} %q_ref.5) | copy-start | bytes 2359300
  0.9 6.0 %collective-permute-start.1 = (bf16[208,256]{1,0:T(8,128)(2,1)S(1)}, bf16[208,256]{1,0:T(8,128)(2,1)S(1)}, u32[]{:S(2)}, u32[]{:S(2)}) collective-permute-start(bf16[208,256]{1,0:T(8,128)(2,1)S(1)} %shard_map.47.refs_0_.own_ref), channel_id=1, source_target_pairs={{2,0},{3,1},{0,2},{1,3},{6,4},{7,5},{4,6},{5,7},{10,8},{11,9},{8,1... | collective-permute-start | bytes 319496 | tf_op jit(solution)/shard_map/ppermute | solution.py:324
  4.8 2.2 %collective-permute-start = (bf16[208,256]{1,0:T(8,128)(2,1)S(1)}, bf16[208,256]{1,0:T(8,128)(2,1)S(1)}, u32[]{:S(2)}, u32[]{:S(2)}) collective-permute-start(bf16[208,256]{1,0:T(8,128)(2,1)S(1)} %shard_map.47.refs_0_.own_ref), channel_id=1, source_target_pairs={{1,0},{0,1},{3,2},{2,3},{5,4},{4,5},{7,6},{6,7},{9,8},{8,9},{11,10... | collective-permute-start | bytes 319496 | tf_op jit(solution)/shard_map/ppermute | solution.py:324
  6.9 1.4 %collective-permute-start.2 = (bf16[208,256]{1,0:T(8,128)(2,1)S(1)}, bf16[208,256]{1,0:T(8,128)(2,1)S(1)}, u32[]{:S(2)}, u32[]{:S(2)}) collective-permute-start(bf16[208,256]{1,0:T(8,128)(2,1)S(1)} %collective-permute-done.1.refs_1_.refs_2_), channel_id=1, source_target_pairs={{1,0},{0,1},{3,2},{2,3},{5,4},{4,5},{7,6},{6,7},{9,8},{8,9},{11,10... | collective-permute-start | bytes 319496 | tf_op jit(solution)/shard_map/ppermute | solution.py:324

commit v6 on v5

--- a/solution.py
+++ b/solution.py
@@ -171,7 +171,6 @@
             pltpu.VMEM((SUMS, keys), bf16),
             pltpu.VMEM((TAIL, keys), bf16),
         ],
-        input_output_aliases={0: 0},
         compiler_params=pltpu.CompilerParams(vmem_limit_bytes=VMEM_LIMIT),
         cost_estimate=pl.CostEstimate(
             flops=4 * rows * heads * keys * HEAD_SIZE,

time: 28.3 us -> 28.1 us (level)
  no operation moved by 1% of the time
where the time goes in v6:
time: 28.1 us; the launch traced here: 28 us
  Pallas kernels  21.9 us (78%)
  starting transfers between devices  3.11 us (11%)
  waiting for transfers between devices  2.08 us (7%)
  local copies, waits for them, and re-layouts  0.85 us (3%)
    pallas_call x1, Pallas kernels, last_part(): pl.pallas_call(functools.partial(last_kernel, held, group_blocks * rows),...  19.8 us
    ppermute x3, starting transfers between devices, swapped(): return lax.ppermute(block, 'ctx', [(i ^ bit, i) for i in devices])  3.11 us
    ppermute x3, waiting for transfers between devices, swapped(): return lax.ppermute(block, 'ctx', [(i ^ bit, i) for i in devices])  2.08 us
    pallas_call x1, Pallas kernels, middle_part(): pl.pallas_call(middle_kernel, out_shape=jax.ShapeDtypeStruct(sums.shape,...  1.29 us
    dynamic_slice x1, local copies, waits for them, and re-layouts, pack(): lax.dynamic_slice_in_dim(a, group * HEAD_SIZE, HEAD_SIZE, 1)  0.84 us
    pallas_call x1, Pallas kernels, first_part(): pl.pallas_call(first_kernel, out_shape=jax.ShapeDtypeStruct((rows // SPAN...  0.81 us
  transfers between devices with their start and end apart: 3, of which 1 were waited for; matrix products, arithmetic and copies ran while one was open for 0% of the time, Pallas kernels for 8%

profile of v6, /device:TPU:0, one launch (start us, length us, event | category | flops | bytes accessed | tf_op | source)
XLA Modules:
  0.0 28.0 jit_solution(11419366832217007574)
XLA Ops:
  0.0 0.0 copy-start.1
  0.0 0.8 %constant_dynamic-slice_fusion = (bf16[192,128]{1,0:T(8,128)(2,1)S(1)}, bf16[192,128]{1,0:T(8,128)(2,1)S(1)}) fusion(bf16[192,1024]{1,0:T(8,128)(2,1)} %param.6, s32[]{:T(128)S(6)} %select_n.10, bf16[192,1024]{1,0:T(8,128)(2,1)} %param.5), kind=kLoop, calls=%fused_computation | loop fusion | bytes 196612 | tf_op jit(solution)/shard_map/dynamic_slice | solution.py:57
  0.8 0.0 copy-done.1
  0.9 0.0 copy-start
  0.9 3.0 %collective-permute-start.1 = (bf16[208,256]{1,0:T(8,128)(2,1)S(1)}, bf16[208,256]{1,0:T(8,128)(2,1)S(1)}, u32[]{:S(2)}, u32[]{:S(2)}) collective-permute-start(bf16[208,256]{1,0:T(8,128)(2,1)S(1)} %shard_map.47.refs_0_.own_ref), channel_id=1, source_target_pairs={{2,0},{3,1},{0,2},{1,3},{6,4},{7,5},{4,6},{5,7},{10,8},{11,9},{8,1... | collective-permute-start | bytes 319496 | tf_op jit(solution)/shard_map/ppermute | solution.py:323
  3.9 0.0 copy-done
  3.9 0.8 %shard_map.48.sums_ref = f32[2,144,1536]{2,1,0:T(8,128)S(1)} custom-call(bf16[192,2048]{1,0:T(8,128)(2,1)S(1)} %copy-done, bf16[208,256]{1,0:T(8,128)(2,1)S(1)} %shard_map.47.refs_0_.own_ref), custom_call_target="tpu_custom_call" | custom-call | flops 301989888 | bytes 1572864 | tf_op jit(solution)/shard_map/pallas_call | solution.py:129
  4.7 0.1 collective-permute-start
  4.8 2.1 %collective-permute-done.1.refs_1_.refs_2_ = bf16[208,256]{1,0:T(8,128)(2,1)S(1)} collective-permute-done((bf16[208,256]{1,0:T(8,128)(2,1)S(1)}, bf16[208,256]{1,0:T(8,128)(2,1)S(1)}, u32[]{:S(2)}, u32[]{:S(2)}) %collective-permute-start.1) | collective-permute-done | bytes 106528 | tf_op jit(solution)/shard_map/ppermute | solution.py:323
  6.9 0.0 collective-permute-start.2
  6.9 0.0 collective-permute-done.refs_0_.refs_1_
  6.9 1.3 %shard_map.49.sums_ref = f32[2,144,1536]{2,1,0:T(8,128)S(1)} custom-call(f32[2,144,1536]{2,1,0:T(8,128)S(1)} %shard_map.48.sums_ref, bf16[192,2048]{1,0:T(8,128)(2,1)S(1)} %copy-done, bf16[208,256]{1,0:T(8,128)(2,1)S(1)} %shard_map.47.refs_0_.own_ref, bf16[208,256]{1,0:T(8,128)(2,1)S(1)} %collective-permute-done.refs_0_.refs_1_, ...), custom_call_target="tpu_custom_call" | custom-call | flops 603979776 | bytes 786432 | tf_op jit(solution)/shard_map/pallas_call | solution.py:164
  8.2 0.0 collective-permute-done.2.refs_3_
  8.2 19.8 %shard_map.50 = bf16[192,2048]{1,0:T(8,128)(2,1)} custom-call(f32[2,144,1536]{2,1,0:T(8,128)S(1)} %shard_map.49.sums_ref, bf16[192,2048]{1,0:T(8,128)(2,1)S(1)} %copy-done, bf16[208,256]{1,0:T(8,128)(2,1)S(1)} %shard_map.47.refs_0_.own_ref, bf16[208,256]{1,0:T(8,128)(2,1)S(1)} %collective-permute-done.refs_0_.refs_1_, ...), custom_call_target="tpu_custom_call" | custom-call | flops 301989888 | bytes 786432 | tf_op jit(solution)/shard_map/pallas_call | solution.py:299
  (2 shorter events, 0.0 us)
Async XLA Ops:
  0.0 0.8 %copy-start.1 = (s32[192]{0:T(256)S(1)}, s32[192]{0:T(256)}, u32[]{:S(2)}) copy-start(s32[192]{0:T(256)} %param.7) | copy-start | bytes 2308
  0.9 3.1 %copy-start = (bf16[192,2048]{1,0:T(8,128)(2,1)S(1)}, bf16[192,2048]{1,0:T(8,128)(2,1)}, u32[]{:S(2)}) copy-start(bf16[192,2048]{1,0:T(8,128)(2,1)} %q_ref.5) | copy-start | bytes 2359300
  0.9 6.0 %collective-permute-start.1 = (bf16[208,256]{1,0:T(8,128)(2,1)S(1)}, bf16[208,256]{1,0:T(8,128)(2,1)S(1)}, u32[]{:S(2)}, u32[]{:S(2)}) collective-permute-start(bf16[208,256]{1,0:T(8,128)(2,1)S(1)} %shard_map.47.refs_0_.own_ref), channel_id=1, source_target_pairs={{2,0},{3,1},{0,2},{1,3},{6,4},{7,5},{4,6},{5,7},{10,8},{11,9},{8,1... | collective-permute-start | bytes 319496 | tf_op jit(solution)/shard_map/ppermute | solution.py:323
  4.7 2.2 %collective-permute-start = (bf16[208,256]{1,0:T(8,128)(2,1)S(1)}, bf16[208,256]{1,0:T(8,128)(2,1)S(1)}, u32[]{:S(2)}, u32[]{:S(2)}) collective-permute-start(bf16[208,256]{1,0:T(8,128)(2,1)S(1)} %shard_map.47.refs_0_.own_ref), channel_id=1, source_target_pairs={{1,0},{0,1},{3,2},{2,3},{5,4},{4,5},{7,6},{6,7},{9,8},{8,9},{11,10... | collective-permute-start | bytes 319496 | tf_op jit(solution)/shard_map/ppermute | solution.py:323
  6.9 1.3 %collective-permute-start.2 = (bf16[208,256]{1,0:T(8,128)(2,1)S(1)}, bf16[208,256]{1,0:T(8,128)(2,1)S(1)}, u32[]{:S(2)}, u32[]{:S(2)}) collective-permute-start(bf16[208,256]{1,0:T(8,128)(2,1)S(1)} %collective-permute-done.1.refs_1_.refs_2_), channel_id=1, source_target_pairs={{1,0},{0,1},{3,2},{2,3},{5,4},{4,5},{7,6},{6,7},{9,8},{8,9},{11,10... | collective-permute-start | bytes 319496 | tf_op jit(solution)/shard_map/ppermute | solution.py:323
